TPU v7x, 32 devices: a whole 2x2x4 slice. The times are simulated.
32 devices in a mesh: seq: 8 (over z, x), exp: 4 (over y, core).
Axes of the slice: x: 2, y: 2, z: 4, core: 2. Of those that a mesh axis runs over, the one named last changes fastest.
Arguments:
- projected: bfloat16 [4, 1024, 3, 4096], P('exp', 'seq'), may hold values from -8 to 8
- patches: bfloat16 [4, 1024, 4096], P('exp', 'seq'), may hold values from -6 to 6
- norm_gain: float32 [4096], replicated, may hold values from 0.1 to 1.9
- expert_ids: int32 [4, 1024, 2], P('exp', 'seq'), may hold values from 0 to 31, all different within a row; in each aligned block of 128 rows (0 to 127, 128 to 255, ..., all dimensions but the last counted through in order) at most 16 rows name the same one
- gate_levels: int32 [4, 1024, 2], P('exp', 'seq'), may hold values from 1 to 256
- w_gate: bfloat16 [32, 4096, 768], P(('seq', 'exp')), may hold values from -0.09375 to 0.09375
- w_up: bfloat16 [32, 4096, 768], P(('seq', 'exp')), may hold values from -0.09375 to 0.09375
- w_down: bfloat16 [32, 768, 4096], P(('seq', 'exp')), may hold values from -0.21875 to 0.21875
Outputs:
- attended: bfloat16 [4, 1024, 4096], P('exp', 'seq')
- layer_out: bfloat16 [4, 1024, 4096], P('exp', 'seq')
Inputs may be any that keep to these rules, and one draw needn't show every extreme that they name: `expert_ids`: each patch names two different experts. Among the 128 patches of one device (aligned blocks of rows, sequences first), at most 16 name the same expert, and in every draw some expert is named by exactly 16 patches of some device.
All inputs are finite; a program needn't handle non-finite values.
Results may differ from a plain program's by a relative error of at most 0.0068.
Values may be sent and summed in bfloat16 or wider, within the bound.
No kernel may reach another device: no remote copies, remote signals or barrier semaphores. Data moves between devices by JAX's collectives and lax.ppermute only.
A program may use at most 128 MiB of HBM per device.

v0:
```python
import math

import jax
import jax.numpy as jnp
from jax import lax
from jax.sharding import PartitionSpec as P

HEADS = 32


def expert_ffn(arrived, w_gate, w_up, w_down):
    flat_rows = arrived.reshape(-1, arrived.shape[-1])
    gate_part = jnp.dot(flat_rows, w_gate[0], preferred_element_type=jnp.float32)
    up_part = jnp.dot(flat_rows, w_up[0], preferred_element_type=jnp.float32)
    hidden = (jax.nn.silu(gate_part) * up_part).astype(jnp.bfloat16)
    result = jnp.dot(hidden, w_down[0], preferred_element_type=jnp.float32).astype(jnp.bfloat16)
    return result.reshape(arrived.shape[:-1] + (w_down.shape[2],))


def shards(projected, patches, norm_gain, expert_ids, gate_levels, w_gate, w_up, w_down):
    seq_count = lax.axis_size("seq")
    exp_count = lax.axis_size("exp")
    tok_rows = patches.shape[1]
    width = patches.shape[2]
    regrouped = lax.all_to_all(projected, "seq", split_axis=3, concat_axis=1, tiled=True)
    length = regrouped.shape[1]
    local_width = regrouped.shape[3]
    local_heads = HEADS // seq_count
    head_width = local_width // local_heads
    scale = 1.0 / math.sqrt(head_width)
    query_rows = regrouped[0, :, 0].reshape(length, local_heads, head_width)
    key_rows = regrouped[0, :, 1].reshape(length, local_heads, head_width)
    value_rows = regrouped[0, :, 2].reshape(length, local_heads, head_width)
    step_rows = min(512, length)

    def attend(block_index):
        start = block_index * step_rows
        query_part = lax.dynamic_slice_in_dim(query_rows, start, step_rows, 0)
        scores = (
            jnp.einsum("qhd,khd->hqk", query_part, key_rows, preferred_element_type=jnp.float32)
            * scale
        )
        query_pos = start + lax.broadcasted_iota(jnp.int32, (step_rows, length), 0)
        key_pos = lax.broadcasted_iota(jnp.int32, (step_rows, length), 1)
        scores = jnp.where((key_pos <= query_pos)[None], scores, jnp.float32(-1e30))
        highest = jnp.max(scores, axis=-1, keepdims=True)
        weights = jnp.exp(scores - highest)
        probs = (weights / jnp.sum(weights, axis=-1, keepdims=True)).astype(jnp.bfloat16)
        mixed_part = jnp.einsum(
            "hqk,khd->qhd", probs, value_rows, preferred_element_type=jnp.float32
        )
        return mixed_part.astype(jnp.bfloat16).reshape(step_rows, local_width)

    outputs = lax.map(attend, jnp.arange(length // step_rows, dtype=jnp.int32))
    head_major = outputs.reshape(1, length, local_width)
    attended = lax.all_to_all(head_major, "seq", split_axis=1, concat_axis=2, tiled=True)
    stream = (patches.astype(jnp.float32) + attended.astype(jnp.float32)).astype(jnp.bfloat16)
    stream_f = stream.astype(jnp.float32)
    mean_square = jnp.mean(stream_f * stream_f, axis=-1, keepdims=True)
    normed = (stream_f * lax.rsqrt(mean_square + 1e-05) * norm_gain).astype(jnp.bfloat16)
    normed_rows = normed[0]
    expert_count = seq_count * exp_count * w_gate.shape[0]
    capacity = max(2, 4 * tok_rows // expert_count)
    routed = expert_ids[0].reshape(-1)
    onehot = (routed[:, None] == jnp.arange(expert_count, dtype=jnp.int32)[None, :]).astype(
        jnp.int32
    )
    slot = jnp.sum(jnp.cumsum(onehot, axis=0) * onehot, axis=1) - 1
    position = routed * capacity + slot
    selection = jnp.arange(expert_count * capacity, dtype=jnp.int32)[:, None] == position[None, :]
    dispatch_matrix = jnp.any(
        selection.reshape(expert_count * capacity, tok_rows, 2), axis=2
    ).astype(jnp.bfloat16)
    buffer = jnp.dot(dispatch_matrix, normed_rows, preferred_element_type=jnp.float32).astype(
        jnp.bfloat16
    )
    outgoing = buffer.reshape(expert_count, capacity, width)
    processed = expert_ffn(
        lax.all_to_all(outgoing, ("seq", "exp"), split_axis=0, concat_axis=0, tiled=True),
        w_gate,
        w_up,
        w_down,
    )
    returned = lax.all_to_all(processed, ("seq", "exp"), split_axis=0, concat_axis=0, tiled=True)
    flat_back = returned.reshape(expert_count * capacity, width)
    picked = flat_back[position].reshape(tok_rows, 2, width).astype(jnp.float32)
    levels = gate_levels[0].astype(jnp.float32)
    share = levels / jnp.sum(levels, axis=-1, keepdims=True)
    mixture = picked[:, 0, :] * share[:, 0:1] + picked[:, 1, :] * share[:, 1:2]
    layer_out = (stream_f[0] + mixture).astype(jnp.bfloat16)
    return (attended, layer_out[None])


def solution(mesh):
    return jax.shard_map(
        shards,
        mesh=mesh,
        in_specs=(
            P("exp", "seq", None, None),
            P("exp", "seq", None),
            P(),
            P("exp", "seq", None),
            P("exp", "seq", None),
            P(("seq", "exp"), None, None),
            P(("seq", "exp"), None, None),
            P(("seq", "exp"), None, None),
        ),
        out_specs=(P("exp", "seq", None), P("exp", "seq", None)),
        check_vma=False,
    )
```

profile of v0, /device:TPU:0, one launch (start us, length us, event | category | flops | bytes accessed | tf_op | source)
XLA Modules:
  0.0 452.3 jit_solution(14695792651133212737)
XLA Ops:
  0.6 7.2 %copy.54 = bf16[1,128,3,4096]{1,2,0,3:T(4,128)(2,1)} copy(bf16[1,128,3,4096]{3,1,2,0:T(8,128)(2,1)} %param.10) | data formatting | bytes 6291456 | tf_op args[0]
  7.8 7.3 %all-to-all-start = ((bf16[1,128,3,4096]{1,2,0,3:T(4,128)(2,1)}), bf16[1,128,3,4096]{1,2,0,3:T(4,128)(2,1)}, u32[]{:S(2)}, u32[]{:S(2)}) async-start(bf16[1,128,3,4096]{1,2,0,3:T(4,128)(2,1)} %copy.54), calls=%async_computation | async-start | bytes 8388608 | tf_op jit(solution)/shard_map/all_to_all | solution.py:25
  15.1 93.3 %all-to-all-done = bf16[1,128,3,4096]{1,2,0,3:T(4,128)(2,1)} async-done(((bf16[1,128,3,4096]{1,2,0,3:T(4,128)(2,1)}), bf16[1,128,3,4096]{1,2,0,3:T(4,128)(2,1)}, u32[]{:S(2)}, u32[]{:S(2)}) %all-to-all-start) | async-done | bytes 3145760 | tf_op jit(solution)/shard_map/all_to_all | solution.py:25
  108.4 4.8 %copy.81 = bf16[1,128,3,8,512]{1,3,4,2,0:T(8,128)(2,1)S(1)} copy(bf16[1,128,3,8,512]{1,2,4,3,0:T(4,128)(2,1)} %bitcast.3) | data formatting | bytes 6291456 | tf_op jit(solution)/shard_map/all_to_all | solution.py:25
  113.1 3.4 all_to_all.35
  116.5 3.8 fusion.55
  120.9 29.5 %while.10 = (s32[]{:T(128)}, bf16[2,512,512]{2,1,0:T(8,128)(2,1)S(1)}, s32[2]{0:T(128)S(1)}, bf16[1024,4,128]{0,2,1:T(8,128)(2,1)}, bf16[1024,4,128]{2,0,1:T(8,1...) while((s32[]{:T(128)}, ...), condition=%wide.region_3.4_spmd, body=%wide.region_0.3_spmd.sunk | while | flops 1087112704 | bytes 23089332 | solution.py:54
  122.6 7.5 %fusion.70 = (f32[4,512]{1,0:T(4,128)S(1)}, f32[4,512,1024]{2,1,0:T(8,128)}) fusion(pred[512,1024]{1,0:T(8,128)(4,1)S(1)} %iota_compare_fusion.5, bf16[1024,4,128]{2,0,1:T(8,128)(2,1)S(1)} %get-tuple-element.153, bf16[1024,4,128]{0,2,1:T(8,128)(2,1)} %get-tuple-element.152, s32[]{:T(128)S(6)} %select_n.32), kind=kOutput, calls=%fused_computation.67.clone.1 | convolution fusion | flops 545260544 | bytes 10493956 | tf_op jit(solution)/shard_map/while/body/eval_jaxpr/sub | solution.py:47
  130.1 5.2 %fusion.71 = bf16[4,512,128]{1,2,0:T(8,128)(2,1)S(1)} fusion(bf16[1024,4,128]{0,2,1:T(8,128)(2,1)} %get-tuple-element.154, f32[4,512,1024]{2,1,0:T(8,128)} %get-tuple-element.127, f32[4,512]{1,0:T(4,128)S(1)} %get-tuple-element.128), kind=kOutput, calls=%fused_computation.11.clone.1 | convolution fusion | flops 541327360 | bytes 9969664 | tf_op jit(solution)/shard_map/while/body/eval_jaxpr/hqk,khd->qhd/dot_general | solution.py:49
  137.2 7.5 %fusion.70 = (f32[4,512]{1,0:T(4,128)S(1)}, f32[4,512,1024]{2,1,0:T(8,128)}) fusion(pred[512,1024]{1,0:T(8,128)(4,1)S(1)} %iota_compare_fusion.5, bf16[1024,4,128]{2,0,1:T(8,128)(2,1)S(1)} %get-tuple-element.153, bf16[1024,4,128]{0,2,1:T(8,128)(2,1)} %get-tuple-element.152, s32[]{:T(128)S(6)} %select_n.32), kind=kOutput, calls=%fused_computation.67.clone.1 | convolution fusion | flops 545260544 | bytes 10493956 | tf_op jit(solution)/shard_map/while/body/eval_jaxpr/sub | solution.py:47
  144.8 5.2 %fusion.71 = bf16[4,512,128]{1,2,0:T(8,128)(2,1)S(1)} fusion(bf16[1024,4,128]{0,2,1:T(8,128)(2,1)} %get-tuple-element.154, f32[4,512,1024]{2,1,0:T(8,128)} %get-tuple-element.127, f32[4,512]{1,0:T(4,128)S(1)} %get-tuple-element.128), kind=kOutput, calls=%fused_computation.11.clone.1 | convolution fusion | flops 541327360 | bytes 9969664 | tf_op jit(solution)/shard_map/while/body/eval_jaxpr/hqk,khd->qhd/dot_general | solution.py:49
  152.6 7.1 %reduce.4 = bf16[1024,512]{1,0:T(8,128)(2,1)S(1)} reduce(bf16[1024,1,512]{2,1,0:T(2,128)(2,1)S(1)} %bitcast.102, bf16[]{:T(256)} %broadcast.146), dimensions={1}, to_apply=%bitcast.88.reduce_sub_computation | reduce | bytes 2097154
  161.2 3.6 all-to-all-start.1
  167.8 23.0 %all-to-all-done.1 = bf16[8,2,32768]{2,1,0:T(2,128)(2,1)S(1)} async-done(((bf16[8,2,32768]{2,1,0:T(2,128)(2,1)}), bf16[8,2,32768]{2,1,0:T(2,128)(2,1)S(1)}, u32[]{:S(2)}, u32[]{:S(2)}) %all-to-all-start.1) | async-done | bytes 1048608 | tf_op jit(solution)/shard_map/all_to_all | solution.py:56
  196.4 97.1 %all_to_all.46 = bf16[32,16,4096]{2,1,0:T(8,128)(2,1)S(1)} all-to-all(bf16[32,16,4096]{2,1,0:T(8,128)(2,1)S(1)} %bitcast.97), channel_id=1, replica_groups=mesh['seq'=8,'exp'=4] {'seq','exp'}, dimensions={0} | all-to-all | bytes 8388608 | tf_op jit(solution)/shard_map/all_to_all | solution.py:79
  295.5 4.6 %fusion.26 = f32[512,768]{1,0:T(8,128)} fusion(bf16[512,4096]{1,0:T(8,128)(2,1)S(1)} %bitcast.105, bf16[1,4096,768]{2,1,0:T(8,128)(2,1)S(1)} %bitcast.114), kind=kOutput, calls=%fused_computation.26 | convolution fusion | flops 3221225472 | bytes 12058624 | tf_op jit(solution)/shard_map/dot_general | solution.py:13
  300.2 17.0 %fusion.28 = bf16[512,4096]{1,0:T(8,128)(2,1)} fusion(bf16[1,768,4096]{2,1,0:T(8,128)(2,1)} %param.17, f32[512,768]{1,0:T(8,128)} %fusion.26, bf16[512,4096]{1,0:T(8,128)(2,1)} %bitcast.106, bf16[1,4096,768]{2,1,0:T(8,128)(2,1)} %param.16), kind=kOutput, calls=%fused_computation.29 | convolution fusion | flops 6446907392 | bytes 22544384 | tf_op jit(solution)/shard_map/dot_general | solution.py:16
  317.1 4.0 all-to-all-start.3
  322.7 92.7 %all-to-all-done.3 = bf16[32,16,4096]{2,1,0:T(8,128)(2,1)} async-done(((bf16[32,16,4096]{2,1,0:T(8,128)(2,1)}), bf16[32,16,4096]{2,1,0:T(8,128)(2,1)}, u32[]{:S(2)}, u32[]{:S(2)}) %all-to-all-start.3) | async-done | bytes 4194336 | tf_op jit(solution)/shard_map/all_to_all | solution.py:84
  415.4 6.6 %gather_fusion = bf16[256,4096]{1,0:T(8,128)(2,1)S(1)} fusion(bf16[512,4096]{1,0:T(8,128)(2,1)} %bitcast.20, s32[1024]{0:T(1024)S(1)} %pad_clamp_fusion), kind=kCustom, calls=%fused_computation | custom fusion | bytes 4195328 | tf_op jit(solution)/shard_map/gather | solution.py:86
  422.0 4.0 reshape.229
  426.0 9.9 %fusion.54 = (f32[128,1,4096]{2,1,0:T(1,128)}, f32[128,1,4096]{2,1,0:T(1,128)}) fusion(f32[128,2,4096]{2,1,0:T(2,128)} %reshape.229), kind=kLoop, calls=%fused_computation.68 | loop fusion | bytes 8388608 | tf_op jit(solution)/shard_map/slice | solution.py:89
  435.9 5.0 %copy.76 = f32[128,1,4096]{0,2,1:T(8,128)S(1)} copy(f32[128,1,4096]{2,1,0:T(1,128)} %get-tuple-element.82) | data formatting | bytes 4194304
  440.9 5.6 %copy.75 = f32[128,1,4096]{0,2,1:T(8,128)} copy(f32[128,1,4096]{2,1,0:T(1,128)} %get-tuple-element.81) | data formatting | bytes 4194304
  (64 shorter events, 24.0 us)
Async XLA Ops:
  7.8 100.6 %all-to-all-start = ((bf16[1,128,3,4096]{1,2,0,3:T(4,128)(2,1)}), bf16[1,128,3,4096]{1,2,0,3:T(4,128)(2,1)}, u32[]{:S(2)}, u32[]{:S(2)}) async-start(bf16[1,128,3,4096]{1,2,0,3:T(4,128)(2,1)} %copy.54), calls=%async_computation | async-start | bytes 8388608 | tf_op jit(solution)/shard_map/all_to_all | solution.py:25
  116.5 4.4 copy-start.1
  152.6 12.3 %copy-start.4 = (s32[1,128,2]{1,2,0:T(2,128)S(1)}, s32[1,128,2]{1,2,0:T(2,128)}, u32[]{:S(2)}) copy-start(s32[1,128,2]{1,2,0:T(2,128)} %param.13) | copy-start | bytes 3076
  159.6 5.6 %copy-start.2 = (bf16[1,128,4096]{2,1,0:T(8,128)(2,1)S(1)}, bf16[1,128,4096]{2,1,0:T(8,128)(2,1)}, u32[]{:S(2)}) copy-start(bf16[1,128,4096]{2,1,0:T(8,128)(2,1)} %param.11) | copy-start | bytes 3145732
  161.2 29.6 %all-to-all-start.1 = ((bf16[8,2,32768]{2,1,0:T(2,128)(2,1)}), bf16[8,2,32768]{2,1,0:T(2,128)(2,1)S(1)}, u32[]{:S(2)}, u32[]{:S(2)}) async-start(bf16[8,2,32768]{2,1,0:T(2,128)(2,1)} %reshape.239), calls=%async_computation.1 | async-start | bytes 2097152 | tf_op jit(solution)/shard_map/all_to_all | solution.py:56
  192.2 2.5 copy-start.3
  194.7 100.8 %slice-start = ((s8[6291456]{0:T(1024)(128)(4,1)}), s8[4194304]{0:T(1024)(128)(4,1)S(1)}, s32[]{:S(2)}) async-start(s8[6291456]{0:T(1024)(128)(4,1)} %bitcast.113), calls=%async_computation.4 | async-start | bytes 8388608
  196.4 99.1 %slice-start.1 = ((s8[6291456]{0:T(1024)(128)(4,1)}), s8[2097152]{0:T(1024)(128)(4,1)S(1)}, s32[]{:S(2)}) async-start(s8[6291456]{0:T(1024)(128)(4,1)} %bitcast.113), calls=%async_computation.5 | async-start | bytes 4194304
  293.5 2.0 copy-start
  317.1 4.2 copy-start.5
  317.1 98.3 %all-to-all-start.3 = ((bf16[32,16,4096]{2,1,0:T(8,128)(2,1)}), bf16[32,16,4096]{2,1,0:T(8,128)(2,1)}, u32[]{:S(2)}, u32[]{:S(2)}) async-start(bf16[32,16,4096]{2,1,0:T(8,128)(2,1)} %bitcast.104), calls=%async_computation.3 | async-start | bytes 8388608 | tf_op jit(solution)/shard_map/all_to_all | solution.py:84
where the time goes:
time: 460 us; the launch traced here: 452 us
  waiting for transfers between devices  209 us (45%)
  blocking collectives  97.1 us (21%)
  local copies, waits for them, and re-layouts  66 us (14%)
  matrix products  48.8 us (11%)
  starting transfers between devices  15 us (3%)
  other arithmetic  13.5 us (3%)
    all_to_all x1, blocking collectives, shards(): lax.all_to_all(outgoing, ('seq', 'exp'), split_axis=0, concat_axis=0, til...  97.1 us
    all_to_all x1, waiting for transfers between devices, shards(): lax.all_to_all(projected, 'seq', split_axis=3, concat_axis=1, tiled=True)  93.3 us
    all_to_all x1, waiting for transfers between devices, shards(): lax.all_to_all(processed, ('seq', 'exp'), split_axis=0, concat_axis=0, ti...  92.7 us
    unnamed x27, local copies, waits for them, and re-layouts  28.3 us
    all_to_all x1, waiting for transfers between devices, shards(): lax.all_to_all(head_major, 'seq', split_axis=1, concat_axis=2, tiled=True)  23 us
    dot_general x1, matrix products, expert_ffn(): jnp.dot(hidden, w_down[0], preferred_element_type=jnp.float32)  17 us
    sub x2, matrix products, attend(): weights = jnp.exp(scores - highest)  15.1 us
    dot_general x2, matrix products, attend(): jnp.einsum('hqk,khd->qhd', probs, value_rows, preferred_element_type=jnp....  10.4 us
  transfers between devices with their start and end apart: 3, of which 3 were waited for; matrix products, arithmetic and copies ran while one was open for 1% of the time, Pallas kernels for 0%

commit v1 on v0

v1 whole, which is shorter than its diff:
```python
import functools
import math

import jax
import jax.numpy as jnp
from jax import lax
from jax.experimental import pallas as pl
from jax.experimental.pallas import tpu as pltpu
from jax.sharding import Mesh
from jax.sharding import PartitionSpec as P

HEADS = 32
SEQ = ("hi", "lo")
HALF = ("lo", "exp")
BF = jnp.bfloat16
F32 = jnp.float32


def attention_kernel(step_rows, qkv_ref, out_ref):
    blocks, _, rows, head_width = qkv_ref.shape
    length = blocks * rows
    factor = math.log2(math.e) / math.sqrt(head_width)
    queries = qkv_ref[:, 0].reshape(length, head_width)
    keys = qkv_ref[:, 1].reshape(length, head_width)
    values = qkv_ref[:, 2].reshape(length, head_width)
    over_width = (((1,), (1,)), ((), ()))
    shape = (step_rows, step_rows)
    seen = lax.broadcasted_iota(jnp.int32, shape, 1) <= lax.broadcasted_iota(jnp.int32, shape, 0)
    for start in range(0, length, step_rows):
        stop = start + step_rows
        part = queries[start:stop]
        near = lax.dot_general(part, keys[start:stop], over_width, preferred_element_type=F32)
        near = jnp.where(seen, near, F32(-1e30))
        highest = jnp.max(near, axis=-1, keepdims=True)
        if start:
            far = lax.dot_general(part, keys[:start], over_width, preferred_element_type=F32)
            highest = jnp.maximum(highest, jnp.max(far, axis=-1, keepdims=True))
        near = jnp.exp2((near - highest) * factor)
        total = jnp.sum(near, axis=-1, keepdims=True)
        mixed = jnp.dot(near.astype(BF), values[start:stop], preferred_element_type=F32)
        if start:
            far = jnp.exp2((far - highest) * factor)
            total += jnp.sum(far, axis=-1, keepdims=True)
            mixed += jnp.dot(far.astype(BF), values[:start], preferred_element_type=F32)
        mixed = (mixed / total).astype(BF)
        for block in range(start // rows, stop // rows):
            low = block * rows - start
            out_ref[block] = mixed[low : low + rows]


def attention(arrived, local_heads):
    blocks, _, rows, local_width = arrived.shape
    head_width = local_width // local_heads
    length = blocks * rows
    return pl.pallas_call(
        functools.partial(attention_kernel, 2 * rows),
        grid=(local_heads,),
        in_specs=[pl.BlockSpec((blocks, 3, rows, head_width), lambda head: (0, 0, 0, head))],
        out_specs=pl.BlockSpec((blocks, rows, head_width), lambda head: (0, 0, head)),
        out_shape=jax.ShapeDtypeStruct((blocks, rows, local_width), BF),
        cost_estimate=pl.CostEstimate(
            flops=2 * length * length * local_width,
            bytes_accessed=8 * length * local_width,
            transcendentals=length * length * local_heads // 2,
        ),
    )(arrived)


def expert_ffn(arrived, w_gate, w_up, w_down):
    rows = arrived.reshape(-1, arrived.shape[-1])
    gate_part = jnp.dot(rows, w_gate[0], preferred_element_type=F32)
    up_part = jnp.dot(rows, w_up[0], preferred_element_type=F32)
    hidden = (jax.nn.silu(gate_part) * up_part).astype(BF)
    result = jnp.dot(hidden, w_down[0], preferred_element_type=F32).astype(BF)
    return result.reshape(arrived.shape)


def routing(expert_ids, gate_levels, first, experts, capacity):
    rows = expert_ids.shape[0]
    routed = expert_ids.reshape(-1)
    names = lax.broadcasted_iota(jnp.int32, (2 * rows, 2 * rows), 1)
    same = (routed[:, None] == routed[None, :]) & (
        names < lax.broadcasted_iota(jnp.int32, (2 * rows, 2 * rows), 0)
    )
    slot = jnp.sum(same.astype(jnp.int32), axis=1)
    local = routed - first
    position = jnp.where((local >= 0) & (local < experts), local * capacity + slot, -1)
    position = position.reshape(rows, 2)
    levels = gate_levels.astype(F32)
    share = levels / jnp.sum(levels, axis=-1, keepdims=True)
    places = lax.broadcasted_iota(jnp.int32, (rows, experts * capacity), 1)
    hit0 = places == position[:, 0:1]
    hit1 = places == position[:, 1:2]
    send = (hit0 | hit1).astype(BF)
    weight = jnp.where(hit0, share[:, 0:1], F32(0)) + jnp.where(hit1, share[:, 1:2], F32(0))
    high = lax.reduce_precision(weight, 8, 7)
    return send, high.astype(BF), (weight - high).astype(BF)


def spread(send, rows):
    return lax.dot_general(
        send, rows, (((0,), (0,)), ((), ())), preferred_element_type=F32
    ).astype(BF)


def gather_back(high, low, rows):
    return jnp.dot(high, rows, preferred_element_type=F32) + jnp.dot(
        low, rows, preferred_element_type=F32
    )


def shards(projected, patches, norm_gain, expert_ids, gate_levels, w_gate, w_up, w_down):
    seq_count = lax.axis_size(SEQ)
    half_count = lax.axis_size(HALF)
    lo_count = lax.axis_size("lo")
    tok_rows = patches.shape[1]
    width = patches.shape[2]
    local_width = width // seq_count
    local_heads = HEADS // seq_count
    expert_count = 2 * half_count
    capacity = max(2, 4 * tok_rows // expert_count)
    mirror = [(i, (i + lo_count) % seq_count) for i in range(seq_count)]
    first = lax.axis_index("hi") * half_count

    def across(value):
        return lax.ppermute(value, SEQ, mirror)

    def exchange(value):
        return lax.all_to_all(value, HALF, split_axis=0, concat_axis=0, tiled=True)

    other_ids = across(expert_ids[0])
    other_levels = across(gate_levels[0])
    own_send, own_high, own_low = routing(
        expert_ids[0], gate_levels[0], first, half_count, capacity
    )
    other_send, other_high, other_low = routing(
        other_ids, other_levels, first, half_count, capacity
    )

    outgoing = jnp.transpose(
        projected[0].reshape(tok_rows, 3, seq_count, local_width), (2, 1, 0, 3)
    )
    arrived = lax.all_to_all(outgoing, SEQ, split_axis=0, concat_axis=0, tiled=True)
    mixed = attention(arrived, local_heads)
    returned = lax.all_to_all(mixed, SEQ, split_axis=0, concat_axis=0, tiled=True)
    attended = jnp.transpose(returned, (1, 0, 2)).reshape(tok_rows, width)
    stream = (patches[0].astype(F32) + attended.astype(F32)).astype(BF)
    stream_f = stream.astype(F32)
    mean_square = jnp.mean(stream_f * stream_f, axis=-1, keepdims=True)
    normed = (stream_f * lax.rsqrt(mean_square + 1e-05) * norm_gain).astype(BF)

    other_normed = across(normed)
    shape = (half_count, capacity, width)
    own_rows = exchange(spread(own_send, normed).reshape(shape))
    own_out = expert_ffn(own_rows, w_gate, w_up, w_down)
    other_rows = exchange(spread(other_send, other_normed).reshape(shape))
    other_out = expert_ffn(other_rows, w_gate, w_up, w_down)
    other_back = exchange(other_out).reshape(-1, width)
    other_part = across(gather_back(other_high, other_low, other_back).astype(BF))
    own_back = exchange(own_out).reshape(-1, width)
    mixture = gather_back(own_high, own_low, own_back) + other_part.astype(F32)
    layer_out = (stream_f + mixture).astype(BF)
    return (attended[None], layer_out[None])


def solution(mesh):
    seq_count, exp_count = mesh.shape["seq"], mesh.shape["exp"]
    finer = Mesh(
        mesh.devices.reshape(2, seq_count // 2, exp_count), ("hi", "lo", "exp")
    )
    tokens = P("exp", SEQ)
    experts = P(("hi", "lo", "exp"), None, None)
    return jax.shard_map(
        shards,
        mesh=finer,
        in_specs=(tokens, tokens, P(), tokens, tokens, experts, experts, experts),
        out_specs=(tokens, tokens),
        check_vma=False,
    )
```

time: 460 us -> 371 us (0.81); the launches traced: 452 us -> 370 us
  local copies, waits for them, and re-layouts: 66 us -> 17 us
  waiting for transfers between devices: 209 us -> 162 us
  blocking collectives: 97.1 us -> 107 us
  other arithmetic: 13.5 us -> 3.92 us
  Pallas kernels: 0 us -> 8.72 us
  starting transfers between devices: 15 us -> 23.6 us
    all_to_all x3 -> x4, waiting for transfers between devices: 209 us -> 51.1 us  [exchange(): return lax.all_to_all(value, HALF, split_axis=0, concat_axis=0, tiled=True)]
    ppermute x0 -> x4, waiting for transfers between devices: none -> 111 us  [across(): return lax.ppermute(value, SEQ, mirror)]
    unnamed x27 -> x11, local copies, waits for them, and re-layouts: 28.3 us -> 7.45 us
    sub x2 -> x0, matrix products: 15.1 us -> none  [attend(): weights = jnp.exp(scores - highest)]
    slice x3 -> x2, local copies, waits for them, and re-layouts: 13.8 us -> 0.35 us  [routing(): hit0 = places == position[:, 0:1]]
    dot_general x5 -> x10, matrix products: 33.7 us -> 46.8 us  [the longest x2 22.6 us: expert_ffn(): result = jnp.dot(hidden, w_down[0], preferred_element_type=F32).astype(BF)]
    all_to_all x1 -> x2, blocking collectives: 97.1 us -> 107 us  [the longest x1 77.9 us: shards(): lax.all_to_all(outgoing, SEQ, split_axis=0, concat_axis=0, tiled=True)]
    all_to_all x3 -> x0, local copies, waits for them, and re-layouts: 8.78 us -> none  [the longest x2 8.12 us: shards(): lax.all_to_all(projected, 'seq', split_axis=3, concat_axis=1, tiled=True)]
  transfers between devices with their start and end apart: 3 -> 8, of which waited for: 3 -> 6; matrix products, arithmetic and copies ran while one was open for 1% -> 12% of each run, Pallas kernels for 0% -> 0%
where the time goes in v1:
time: 371 us; the launch traced here: 370 us
  waiting for transfers between devices  162 us (44%)
  blocking collectives  107 us (29%)
  matrix products  46.8 us (13%)
  starting transfers between devices  23.6 us (6%)
  local copies, waits for them, and re-layouts  17 us (5%)
  Pallas kernels  8.72 us (2%)
  other arithmetic  3.92 us (1%)
    ppermute x4, waiting for transfers between devices, across(): return lax.ppermute(value, SEQ, mirror)  111 us
    all_to_all x1, blocking collectives, shards(): lax.all_to_all(outgoing, SEQ, split_axis=0, concat_axis=0, tiled=True)  77.9 us
    all_to_all x4, waiting for transfers between devices, exchange(): return lax.all_to_all(value, HALF, split_axis=0, concat_axis=0, tiled=True)  51.1 us
    all_to_all x1, blocking collectives, shards(): lax.all_to_all(mixed, SEQ, split_axis=0, concat_axis=0, tiled=True)  29.2 us
    dot_general x2, matrix products, expert_ffn(): result = jnp.dot(hidden, w_down[0], preferred_element_type=F32).astype(BF)  22.6 us
    all_to_all x4, starting transfers between devices, exchange(): return lax.all_to_all(value, HALF, split_axis=0, concat_axis=0, tiled=True)  16.6 us
    dot_general x2, matrix products, expert_ffn(): gate_part = jnp.dot(rows, w_gate[0], preferred_element_type=F32)  12.2 us
    pallas_call x1, Pallas kernels, attention(): pl.pallas_call(functools.partial(attention_kernel, 2 * rows), grid=(local...  8.72 us
  transfers between devices with their start and end apart: 8, of which 6 were waited for; matrix products, arithmetic and copies ran while one was open for 12% of the time, Pallas kernels for 0%

profile of v1, /device:TPU:0, one launch (start us, length us, event | category | flops | bytes accessed | tf_op | source)
XLA Modules:
  0.0 370.1 jit_solution(17725009500227896411)
XLA Ops:
  0.6 4.7 %copy.26 = bf16[1,128,3,4096]{1,3,2,0:T(8,128)(2,1)} copy(bf16[1,128,3,4096]{3,1,2,0:T(8,128)(2,1)} %param.8) | data formatting | bytes 6291456 | tf_op args[0]
  5.3 3.2 copy.27
  8.5 77.9 %all_to_all.30.qkv_ref = bf16[8,3,128,512]{3,2,1,0:T(8,128)(2,1)} all-to-all(bf16[8,3,128,512]{3,2,1,0:T(8,128)(2,1)S(1)} %bitcast.76), channel_id=1, replica_groups=mesh['hi'=2,'lo'=4,'exp'=4] {'hi','lo'}, dimensions={0} | all-to-all | bytes 6291456 | tf_op jit(solution)/shard_map/all_to_all | solution.py:143
  86.4 8.7 %shard_map.95 = bf16[8,128,512]{2,1,0:T(8,128)(2,1)} custom-call(bf16[8,3,128,512]{3,2,1,0:T(8,128)(2,1)} %all_to_all.30.qkv_ref), custom_call_target="tpu_custom_call" | custom-call | flops 1073741824 | bytes 4194304 | tf_op jit(solution)/shard_map/pallas_call | solution.py:55
  95.1 29.2 %all_to_all.31 = bf16[8,128,512]{2,1,0:T(8,128)(2,1)} all-to-all(bf16[8,128,512]{2,1,0:T(8,128)(2,1)} %shard_map.95), channel_id=1, replica_groups=mesh['hi'=2,'lo'=4,'exp'=4] {'hi','lo'}, dimensions={0} | all-to-all | bytes 2097152 | tf_op jit(solution)/shard_map/all_to_all | solution.py:145
  134.8 46.7 %collective-permute-done = s32[128,2]{1,0:T(8,128)S(1)} collective-permute-done((s32[128,2]{1,0:T(8,128)S(1)}, s32[128,2]{1,0:T(8,128)S(1)}, u32[]{:S(2)}, u32[]{:S(2)}) %collective-permute-start) | collective-permute-done | bytes 1056 | tf_op jit(solution)/shard_map/ppermute | solution.py:126
  182.2 2.2 convolution_convert_fusion
  184.3 4.4 %all-to-all-start.4 = ((bf16[16,16,4096]{2,1,0:T(8,128)(2,1)}), bf16[16,16,4096]{2,1,0:T(8,128)(2,1)}, u32[]{:S(2)}, u32[]{:S(2)}) async-start(bf16[16,16,4096]{2,1,0:T(8,128)(2,1)} %bitcast.19), calls=%async_computation.4 | async-start | bytes 4194304 | tf_op jit(solution)/shard_map/all_to_all | solution.py:129
  189.5 2.2 convolution_convert_fusion.1
  191.6 26.8 %all-to-all-done.4 = bf16[16,16,4096]{2,1,0:T(8,128)(2,1)} async-done(((bf16[16,16,4096]{2,1,0:T(8,128)(2,1)}), bf16[16,16,4096]{2,1,0:T(8,128)(2,1)}, u32[]{:S(2)}, u32[]{:S(2)}) %all-to-all-start.4) | async-done | bytes 2097184 | tf_op jit(solution)/shard_map/all_to_all | solution.py:129
  218.5 3.7 %all-to-all-start.2 = ((bf16[16,16,4096]{2,1,0:T(8,128)(2,1)}), bf16[16,16,4096]{2,1,0:T(8,128)(2,1)S(1)}, u32[]{:S(2)}, u32[]{:S(2)}) async-start(bf16[16,16,4096]{2,1,0:T(8,128)(2,1)} %bitcast.10), calls=%async_computation.2 | async-start | bytes 4194304 | tf_op jit(solution)/shard_map/all_to_all | solution.py:129
  222.2 6.1 %fusion.8 = f32[256,768]{1,0:T(8,128)} fusion(bf16[256,4096]{1,0:T(8,128)(2,1)} %bitcast.20, bf16[1,4096,768]{2,1,0:T(8,128)(2,1)} %param.13), kind=kOutput, calls=%fused_computation.8 | convolution fusion | flops 1610612736 | bytes 9175040 | tf_op jit(solution)/shard_map/dot_general | solution.py:71
  228.3 11.3 %fusion.15 = bf16[256,4096]{1,0:T(8,128)(2,1)} fusion(bf16[1,768,4096]{2,1,0:T(8,128)(2,1)} %param.15, bf16[256,4096]{1,0:T(8,128)(2,1)} %bitcast.20, bf16[1,4096,768]{2,1,0:T(8,128)(2,1)} %param.14, f32[256,768]{1,0:T(8,128)} %fusion.8), kind=kOutput, calls=%fused_computation.15 | convolution fusion | flops 3223453696 | bytes 17563648 | tf_op jit(solution)/shard_map/dot_general | solution.py:74
  239.6 12.2 %all-to-all-done.2 = bf16[16,16,4096]{2,1,0:T(8,128)(2,1)S(1)} async-done(((bf16[16,16,4096]{2,1,0:T(8,128)(2,1)}), bf16[16,16,4096]{2,1,0:T(8,128)(2,1)S(1)}, u32[]{:S(2)}, u32[]{:S(2)}) %all-to-all-start.2) | async-done | bytes 2097184 | tf_op jit(solution)/shard_map/all_to_all | solution.py:129
  253.2 3.9 %all-to-all-start.5 = ((bf16[16,16,4096]{2,1,0:T(8,128)(2,1)}), bf16[16,16,4096]{2,1,0:T(8,128)(2,1)S(1)}, u32[]{:S(2)}, u32[]{:S(2)}) async-start(bf16[16,16,4096]{2,1,0:T(8,128)(2,1)} %bitcast.83), calls=%async_computation.5 | async-start | bytes 4194304 | tf_op jit(solution)/shard_map/all_to_all | solution.py:129
  257.1 6.1 %fusion.10 = f32[256,768]{1,0:T(8,128)} fusion(bf16[256,4096]{1,0:T(8,128)(2,1)} %bitcast.81, bf16[1,4096,768]{2,1,0:T(8,128)(2,1)} %param.13), kind=kOutput, calls=%fused_computation.10 | convolution fusion | flops 1610612736 | bytes 9175040 | tf_op jit(solution)/shard_map/dot_general | solution.py:71
  263.1 11.3 %fusion.12 = bf16[256,4096]{1,0:T(8,128)(2,1)} fusion(bf16[1,768,4096]{2,1,0:T(8,128)(2,1)} %param.15, bf16[256,4096]{1,0:T(8,128)(2,1)} %bitcast.82, bf16[1,4096,768]{2,1,0:T(8,128)(2,1)} %param.14, f32[256,768]{1,0:T(8,128)} %fusion.10), kind=kOutput, calls=%fused_computation.14 | convolution fusion | flops 3223453696 | bytes 17563648 | tf_op jit(solution)/shard_map/dot_general | solution.py:74
  274.4 12.1 %all-to-all-done.5 = bf16[16,16,4096]{2,1,0:T(8,128)(2,1)S(1)} async-done(((bf16[16,16,4096]{2,1,0:T(8,128)(2,1)}), bf16[16,16,4096]{2,1,0:T(8,128)(2,1)S(1)}, u32[]{:S(2)}, u32[]{:S(2)}) %all-to-all-start.5) | async-done | bytes 2097184 | tf_op jit(solution)/shard_map/all_to_all | solution.py:129
  286.5 4.6 %all-to-all-start.3 = ((bf16[16,16,4096]{2,1,0:T(8,128)(2,1)}), bf16[16,16,4096]{2,1,0:T(8,128)(2,1)}, u32[]{:S(2)}, u32[]{:S(2)}) async-start(bf16[16,16,4096]{2,1,0:T(8,128)(2,1)} %bitcast.80), calls=%async_computation.3 | async-start | bytes 4194304 | tf_op jit(solution)/shard_map/all_to_all | solution.py:129
  291.7 24.2 %collective-permute-done.1 = s32[128,2]{0,1:T(2,128)S(1)} collective-permute-done((s32[128,2]{0,1:T(2,128)S(1)}, s32[128,2]{0,1:T(2,128)S(1)}, u32[]{:S(2)}, u32[]{:S(2)}) %collective-permute-start.1) | collective-permute-done | bytes 1056 | tf_op jit(solution)/shard_map/ppermute | solution.py:126
  318.0 3.3 collective-permute-start.3
  324.2 2.1 fusion.55
  326.3 40.3 %collective-permute-done.3 = bf16[128,4096]{1,0:T(8,128)(2,1)S(1)} collective-permute-done((bf16[128,4096]{1,0:T(8,128)(2,1)}, bf16[128,4096]{1,0:T(8,128)(2,1)S(1)}, u32[]{:S(2)}, u32[]{:S(2)}) %collective-permute-start.3) | collective-permute-done | bytes 1048608 | tf_op jit(solution)/shard_map/ppermute | solution.py:126
  366.6 3.5 fusion.36
  (40 shorter events, 18.7 us)
Async XLA Ops:
  129.6 1.7 copy-start.1
  131.2 1.5 copy-start.2
  131.6 50.5 %collective-permute-start.2 = (bf16[128,4096]{1,0:T(8,128)(2,1)S(1)}, bf16[128,4096]{1,0:T(8,128)(2,1)S(1)}, u32[]{:S(2)}, u32[]{:S(2)}) collective-permute-start(bf16[128,4096]{1,0:T(8,128)(2,1)S(1)} %fusion.21), channel_id=1, source_target_pairs={{0,16},{4,20},{8,24},{12,28},{16,0},{20,4},{24,8},{28,12},{1,17},{... | collective-permute-start | bytes 3145736 | tf_op jit(solution)/shard_map/ppermute | solution.py:126
  132.8 48.7 %collective-permute-start = (s32[128,2]{1,0:T(8,128)S(1)}, s32[128,2]{1,0:T(8,128)S(1)}, u32[]{:S(2)}, u32[]{:S(2)}) collective-permute-start(s32[128,2]{1,0:T(8,128)S(1)} %bitcast.84), channel_id=1, source_target_pairs={{0,16},{4,20},{8,24},{12,28},{16,0},{20,4},{24,8},{28,12},{1,17},{... | collective-permute-start | bytes 3080 | tf_op jit(solution)/shard_map/ppermute | solution.py:126
  184.3 34.1 %all-to-all-start.4 = ((bf16[16,16,4096]{2,1,0:T(8,128)(2,1)}), bf16[16,16,4096]{2,1,0:T(8,128)(2,1)}, u32[]{:S(2)}, u32[]{:S(2)}) async-start(bf16[16,16,4096]{2,1,0:T(8,128)(2,1)} %bitcast.19), calls=%async_computation.4 | async-start | bytes 4194304 | tf_op jit(solution)/shard_map/all_to_all | solution.py:129
  218.5 33.4 %all-to-all-start.2 = ((bf16[16,16,4096]{2,1,0:T(8,128)(2,1)}), bf16[16,16,4096]{2,1,0:T(8,128)(2,1)S(1)}, u32[]{:S(2)}, u32[]{:S(2)}) async-start(bf16[16,16,4096]{2,1,0:T(8,128)(2,1)} %bitcast.10), calls=%async_computation.2 | async-start | bytes 4194304 | tf_op jit(solution)/shard_map/all_to_all | solution.py:129
  251.8 1.3 copy-start
  253.2 33.4 %all-to-all-start.5 = ((bf16[16,16,4096]{2,1,0:T(8,128)(2,1)}), bf16[16,16,4096]{2,1,0:T(8,128)(2,1)S(1)}, u32[]{:S(2)}, u32[]{:S(2)}) async-start(bf16[16,16,4096]{2,1,0:T(8,128)(2,1)} %bitcast.83), calls=%async_computation.5 | async-start | bytes 4194304 | tf_op jit(solution)/shard_map/all_to_all | solution.py:129
  286.5 4.6 %copy-start.3 = (s32[1,128,2]{1,2,0:T(2,128)S(1)}, s32[1,128,2]{1,2,0:T(2,128)}, u32[]{:S(2)}) copy-start(s32[1,128,2]{1,2,0:T(2,128)} %param.12) | copy-start | bytes 3076
  286.5 37.7 %all-to-all-start.3 = ((bf16[16,16,4096]{2,1,0:T(8,128)(2,1)}), bf16[16,16,4096]{2,1,0:T(8,128)(2,1)}, u32[]{:S(2)}, u32[]{:S(2)}) async-start(bf16[16,16,4096]{2,1,0:T(8,128)(2,1)} %bitcast.80), calls=%async_computation.3 | async-start | bytes 4194304 | tf_op jit(solution)/shard_map/all_to_all | solution.py:129
  291.1 24.8 %collective-permute-start.1 = (s32[128,2]{0,1:T(2,128)S(1)}, s32[128,2]{0,1:T(2,128)S(1)}, u32[]{:S(2)}, u32[]{:S(2)}) collective-permute-start(s32[128,2]{0,1:T(2,128)S(1)} %bitcast.85), channel_id=1, source_target_pairs={{0,16},{4,20},{8,24},{12,28},{16,0},{20,4},{24,8},{28,12},{1,17},{... | collective-permute-start | bytes 3080 | tf_op jit(solution)/shard_map/ppermute | solution.py:126
  318.0 48.6 %collective-permute-start.3 = (bf16[128,4096]{1,0:T(8,128)(2,1)}, bf16[128,4096]{1,0:T(8,128)(2,1)S(1)}, u32[]{:S(2)}, u32[]{:S(2)}) collective-permute-start(bf16[128,4096]{1,0:T(8,128)(2,1)} %fusion.18), channel_id=1, source_target_pairs={{0,16},{4,20},{8,24},{12,28},{16,0},{20,4},{24,8},{28,12},{1,17},{... | collective-permute-start | bytes 3145736 | tf_op jit(solution)/shard_map/ppermute | solution.py:126

commit v2 on v1

--- a/solution.py
+++ b/solution.py
@@ -8,6 +8,7 @@
 from jax.experimental.pallas import tpu as pltpu
 from jax.sharding import Mesh
 from jax.sharding import PartitionSpec as P
+
 
 HEADS = 32
 SEQ = ("hi", "lo")
@@ -57,7 +58,8 @@
         grid=(local_heads,),
         in_specs=[pl.BlockSpec((blocks, 3, rows, head_width), lambda head: (0, 0, 0, head))],
         out_specs=pl.BlockSpec((blocks, rows, head_width), lambda head: (0, 0, head)),
-        out_shape=jax.ShapeDtypeStruct((blocks, rows, local_width), BF),
+        out_shape=pltpu.HBM((blocks, rows, local_width), BF),
+        compiler_params=pltpu.CompilerParams(vmem_limit_bytes=20 << 20),
         cost_estimate=pl.CostEstimate(
             flops=2 * length * length * local_width,
             bytes_accessed=8 * length * local_width,
@@ -66,13 +68,155 @@
     )(arrived)
 
 
-def expert_ffn(arrived, w_gate, w_up, w_down):
-    rows = arrived.reshape(-1, arrived.shape[-1])
-    gate_part = jnp.dot(rows, w_gate[0], preferred_element_type=F32)
-    up_part = jnp.dot(rows, w_up[0], preferred_element_type=F32)
-    hidden = (jax.nn.silu(gate_part) * up_part).astype(BF)
-    result = jnp.dot(hidden, w_down[0], preferred_element_type=F32).astype(BF)
-    return result.reshape(arrived.shape)
+def expert_kernel(rows_ref, gate_hbm, up_hbm, down_hbm, out_ref, gate_ref, up_ref, down_ref, hidden_ref, arrived):
+    pieces = arrived.shape[1]
+    weights = ((gate_hbm, gate_ref), (up_hbm, up_ref), (down_hbm, down_ref))
+    copies = []
+    for kind, (source, target) in enumerate(weights):
+        depth = target.shape[0] // pieces
+        group = []
+        for piece in range(pieces):
+            part = pl.ds(piece * depth, depth)
+            group.append(
+                pltpu.make_async_copy(source.at[0, part], target.at[part], arrived.at[kind, piece])
+            )
+        copies.append(group)
+    for copy in copies[0] + copies[1] + copies[2]:
+        copy.start()
+
+    def columns_of(width, most):
+        tile = math.gcd(width, most)
+        return [slice(start, start + tile) for start in range(0, width, tile)]
+
+    rows = rows_ref[...]
+    for copy in copies[0]:
+        copy.wait()
+    gates = []
+    for columns in columns_of(gate_ref.shape[1], 256):
+        gates.append(jnp.dot(rows, gate_ref[:, columns], preferred_element_type=F32))
+    for copy in copies[1]:
+        copy.wait()
+    for gate, columns in zip(gates, columns_of(gate_ref.shape[1], 256)):
+        up = jnp.dot(rows, up_ref[:, columns], preferred_element_type=F32)
+        hidden_ref[:, columns] = (gate / (1.0 + jnp.exp(-gate)) * up).astype(BF)
+    hidden_rows = hidden_ref[...]
+    for copy in copies[2]:
+        copy.wait()
+    for columns in columns_of(down_ref.shape[1], 512):
+        out_ref[:, columns] = jnp.dot(
+            hidden_rows, down_ref[:, columns], preferred_element_type=F32
+        ).astype(BF)
+
+
+def in_hbm(array):
+    return pltpu.with_memory_space_constraint(array, pltpu.HBM)
+
+
+def expert_ffn(rows, w_gate, w_up, w_down):
+    count, width = rows.shape
+    hidden = w_gate.shape[2]
+    vmem = pl.BlockSpec(memory_space=pltpu.VMEM)
+    hbm = pl.BlockSpec(memory_space=pltpu.HBM)
+    return pl.pallas_call(
+        expert_kernel,
+        in_specs=[vmem, hbm, hbm, hbm],
+        out_specs=vmem,
+        out_shape=jax.ShapeDtypeStruct((count, width), BF),
+        scratch_shapes=[
+            pltpu.VMEM((width, hidden), BF),
+            pltpu.VMEM((width, hidden), BF),
+            pltpu.VMEM((hidden, width), BF),
+            pltpu.VMEM((count, hidden), BF),
+            pltpu.SemaphoreType.DMA((3, 4)),
+        ],
+        compiler_params=pltpu.CompilerParams(vmem_limit_bytes=30 << 20),
+        cost_estimate=pl.CostEstimate(
+            flops=6 * count * width * hidden,
+            bytes_accessed=6 * width * hidden + 4 * count * width,
+            transcendentals=count * hidden,
+        ),
+    )(rows, in_hbm(w_gate), in_hbm(w_up), in_hbm(w_down))
+
+
+def regroup_kernel(in_ref, out_ref, held, arrived, left):
+    blocks, _, _, local_width = held.shape
+    reads, writes = [], []
+    for block in range(blocks):
+        columns = pl.ds(block * local_width, local_width)
+        reads.append(
+            pltpu.make_async_copy(in_ref.at[:, :, columns], held.at[block], arrived.at[block])
+        )
+        writes.append(pltpu.make_async_copy(held.at[block], out_ref.at[block], left.at[block]))
+    for read in reads:
+        read.start()
+    for read, write in zip(reads, writes):
+        read.wait()
+        write.start()
+    for write in writes:
+        write.wait()
+
+
+def regroup(projected, blocks):
+    kinds, rows, width = projected.shape
+    shape = (blocks, kinds, rows, width // blocks)
+    hbm = pl.BlockSpec(memory_space=pltpu.HBM)
+    return pl.pallas_call(
+        regroup_kernel,
+        in_specs=[hbm],
+        out_specs=hbm,
+        out_shape=pltpu.HBM(shape, BF),
+        scratch_shapes=[
+            pltpu.VMEM(shape, BF),
+            pltpu.SemaphoreType.DMA((blocks,)),
+            pltpu.SemaphoreType.DMA((blocks,)),
+        ],
+        compiler_params=pltpu.CompilerParams(vmem_limit_bytes=59 << 20),
+    )(projected)
+
+
+def norm_kernel(parts, *refs):
+    returned, (patches_ref, gain_ref, attended_ref, stream_ref) = refs[:parts], refs[parts:parts + 4]
+    normed_refs = refs[parts + 4 :]
+    blocks, _, part_width = returned[0].shape
+    total = 0.0
+    for block in range(blocks * parts):
+        columns = slice(block * part_width, (block + 1) * part_width)
+        part = returned[block % parts][block // parts]
+        attended_ref[:, columns] = part
+        stream = (patches_ref[:, columns].astype(F32) + part.astype(F32)).astype(BF)
+        stream_ref[:, columns] = stream
+        stream_f = stream.astype(F32)
+        total += jnp.sum(stream_f * stream_f, axis=-1, keepdims=True)
+    factor = lax.rsqrt(total / (blocks * parts * part_width) + 1e-05)
+    start = 0
+    for normed_ref in normed_refs:
+        stop = start + normed_ref.shape[1]
+        stream_f = stream_ref[:, start:stop].astype(F32)
+        normed_ref[...] = (stream_f * factor * gain_ref[:, start:stop]).astype(BF)
+        start = stop
+
+
+def residual_norm(returned, patches, gain, chunks):
+    blocks, rows, part_width = returned[0].shape
+    width = patches.shape[1]
+    tile = math.gcd(rows, 32)
+    at = lambda step: (step, 0)
+    shape = lambda columns: jax.ShapeDtypeStruct((rows, columns), BF)
+    return pl.pallas_call(
+        functools.partial(norm_kernel, len(returned)),
+        grid=(rows // tile,),
+        in_specs=[
+            pl.BlockSpec((blocks, tile, part_width), lambda step: (0, step, 0)) for _ in returned
+        ]
+        + [
+            pl.BlockSpec((tile, width), at),
+            pl.BlockSpec((1, width), lambda step: (0, 0)),
+        ],
+        out_specs=[pl.BlockSpec((tile, width), at)] * 2
+        + [pl.BlockSpec((tile, width // chunks), at)] * chunks,
+        out_shape=[pltpu.HBM((rows, width), BF)] * 2 + [shape(width // chunks)] * chunks,
+        compiler_params=pltpu.CompilerParams(vmem_limit_bytes=8 << 20),
+    )(*returned, patches, gain)
 
 
 def routing(expert_ids, gate_levels, first, experts, capacity):
@@ -114,8 +258,6 @@
     half_count = lax.axis_size(HALF)
     lo_count = lax.axis_size("lo")
     tok_rows = patches.shape[1]
-    width = patches.shape[2]
-    local_width = width // seq_count
     local_heads = HEADS // seq_count
     expert_count = 2 * half_count
     capacity = max(2, 4 * tok_rows // expert_count)
@@ -125,41 +267,36 @@
     def across(value):
         return lax.ppermute(value, SEQ, mirror)
 
-    def exchange(value):
-        return lax.all_to_all(value, HALF, split_axis=0, concat_axis=0, tiled=True)
-
-    other_ids = across(expert_ids[0])
-    other_levels = across(gate_levels[0])
+    def exchange(axes, value):
+        return lax.all_to_all(value, axes, split_axis=0, concat_axis=0, tiled=True)
+
+    def routed(value):
+        sent = value.reshape(half_count, capacity, value.shape[1])
+        return exchange(HALF, sent).reshape(value.shape)
+
+    other = across(jnp.concatenate([expert_ids[0], gate_levels[0]], axis=1))
+    outgoing = regroup(jnp.transpose(projected[0], (1, 0, 2)), seq_count)
+    arrived = exchange(SEQ, outgoing)
+    arrived, other = lax.optimization_barrier((arrived, other))
     own_send, own_high, own_low = routing(
         expert_ids[0], gate_levels[0], first, half_count, capacity
     )
     other_send, other_high, other_low = routing(
-        other_ids, other_levels, first, half_count, capacity
-    )
-
-    outgoing = jnp.transpose(
-        projected[0].reshape(tok_rows, 3, seq_count, local_width), (2, 1, 0, 3)
-    )
-    arrived = lax.all_to_all(outgoing, SEQ, split_axis=0, concat_axis=0, tiled=True)
-    mixed = attention(arrived, local_heads)
-    returned = lax.all_to_all(mixed, SEQ, split_axis=0, concat_axis=0, tiled=True)
-    attended = jnp.transpose(returned, (1, 0, 2)).reshape(tok_rows, width)
-    stream = (patches[0].astype(F32) + attended.astype(F32)).astype(BF)
-    stream_f = stream.astype(F32)
-    mean_square = jnp.mean(stream_f * stream_f, axis=-1, keepdims=True)
-    normed = (stream_f * lax.rsqrt(mean_square + 1e-05) * norm_gain).astype(BF)
+        other[:, :2], other[:, 2:], first, half_count, capacity
+    )
+    returned = [exchange(SEQ, attention(arrived, local_heads))]
+    attended, stream, normed = residual_norm(returned, patches[0], norm_gain[None], 1)
 
     other_normed = across(normed)
-    shape = (half_count, capacity, width)
-    own_rows = exchange(spread(own_send, normed).reshape(shape))
+    own_rows = routed(spread(own_send, normed))
+    other_rows = routed(spread(other_send, other_normed))
     own_out = expert_ffn(own_rows, w_gate, w_up, w_down)
-    other_rows = exchange(spread(other_send, other_normed).reshape(shape))
     other_out = expert_ffn(other_rows, w_gate, w_up, w_down)
-    other_back = exchange(other_out).reshape(-1, width)
+    other_back = routed(other_out)
     other_part = across(gather_back(other_high, other_low, other_back).astype(BF))
-    own_back = exchange(own_out).reshape(-1, width)
-    mixture = gather_back(own_high, own_low, own_back) + other_part.astype(F32)
-    layer_out = (stream_f + mixture).astype(BF)
+    own_back = routed(own_out)
+    own_total = stream.astype(F32) + gather_back(own_high, own_low, own_back)
+    layer_out = (own_total + other_part.astype(F32)).astype(BF)
     return (attended[None], layer_out[None])
 
 

time: 371 us -> 335 us (0.903)
  blocking collectives: 107 us -> 29.7 us
  waiting for transfers between devices: 162 us -> 225 us
  matrix products: 46.8 us -> 11.1 us
  Pallas kernels: 8.72 us -> 34.6 us
  local copies, waits for them, and re-layouts: 17 us -> 2.8 us
  starting transfers between devices: 23.6 us -> 29.4 us
    all_to_all x2 -> x1, blocking collectives: 107 us -> 29.7 us  [exchange(): return lax.all_to_all(value, axes, split_axis=0, concat_axis=0, tiled=True)]
    all_to_all x4 -> x5, waiting for transfers between devices: 51.1 us -> 109 us  [exchange(): return lax.all_to_all(value, axes, split_axis=0, concat_axis=0, tiled=True)]
    dot_general x4 -> x0, matrix products: 34.8 us -> none  [the longest x2 22.6 us: expert_ffn(): result = jnp.dot(hidden, w_down[0], preferred_element_type=F32).astype(BF)]
    pallas_call x0 -> x4, Pallas kernels: none -> 26.5 us  [the longest x2 21.7 us: expert_ffn(): pl.pallas_call(expert_kernel, in_specs=[vmem, hbm, hbm, hbm], out_specs=v...]
    all_to_all x4 -> x5, starting transfers between devices: 16.6 us -> 23.8 us  [exchange(): return lax.all_to_all(value, axes, split_axis=0, concat_axis=0, tiled=True)]
    unnamed x11 -> x14, local copies, waits for them, and re-layouts: 7.45 us -> 1.54 us
    ppermute x4 -> x3, waiting for transfers between devices: 111 us -> 115 us  [across(): return lax.ppermute(value, SEQ, mirror)]
    convert_element_type x2 -> x0, local copies, waits for them, and re-layouts: 3.79 us -> none  [shards(): stream = (patches[0].astype(F32) + attended.astype(F32)).astype(BF)]
  transfers between devices with their start and end apart: 8 -> 8, of which waited for: 6 -> 6; matrix products, arithmetic and copies ran while one was open for 12% -> 2% of each run, Pallas kernels for 0% -> 6%
where the time goes in v2:
time: 335 us; the launch traced here: 334 us
  waiting for transfers between devices  225 us (67%)
  Pallas kernels  34.6 us (10%)
  blocking collectives  29.7 us (9%)
  starting transfers between devices  29.4 us (9%)
  matrix products  11.1 us (3%)
    ppermute x3, waiting for transfers between devices, across(): return lax.ppermute(value, SEQ, mirror)  115 us
    all_to_all x5, waiting for transfers between devices, exchange(): return lax.all_to_all(value, axes, split_axis=0, concat_axis=0, tiled=True)  109 us
    all_to_all x1, blocking collectives, exchange(): return lax.all_to_all(value, axes, split_axis=0, concat_axis=0, tiled=True)  29.7 us
    all_to_all x5, starting transfers between devices, exchange(): return lax.all_to_all(value, axes, split_axis=0, concat_axis=0, tiled=True)  23.8 us
    pallas_call x2, Pallas kernels, expert_ffn(): pl.pallas_call(expert_kernel, in_specs=[vmem, hbm, hbm, hbm], out_specs=v...  21.7 us
    pallas_call x1, Pallas kernels, attention(): pl.pallas_call(functools.partial(attention_kernel, 2 * rows), grid=(local...  8.15 us
  transfers between devices with their start and end apart: 8, of which 6 were waited for; matrix products, arithmetic and copies ran while one was open for 2% of the time, Pallas kernels for 6%

profile of v2, /device:TPU:0, one launch (start us, length us, event | category | flops | bytes accessed | tf_op | source)
XLA Modules:
  0.0 334.2 jit_solution(15245016756128035125)
XLA Ops:
  0.6 2.8 shard_map.95
  3.5 7.3 %all-to-all-start = ((bf16[8,3,128,512]{3,2,1,0:T(8,128)(2,1)}), bf16[8,3,128,512]{3,2,1,0:T(8,128)(2,1)S(1)}, u32[]{:S(2)}, u32[]{:S(2)}) async-start(bf16[8,3,128,512]{3,2,1,0:T(8,128)(2,1)} %shard_map.95), calls=%async_computation | async-start | bytes 6291456 | tf_op jit(solution)/shard_map/all_to_all | solution.py:271
  11.1 3.0 collective-permute-start
  14.1 70.2 %collective-permute-done = s32[128,4]{1,0:T(8,128)S(1)} collective-permute-done((s32[128,4]{1,0:T(8,128)S(1)}, s32[128,4]{1,0:T(8,128)S(1)}, u32[]{:S(2)}, u32[]{:S(2)}) %collective-permute-start) | collective-permute-done | bytes 2080 | tf_op jit(solution)/shard_map/ppermute | solution.py:268
  84.3 8.1 %shard_map.96 = bf16[8,128,512]{2,1,0:T(8,128)(2,1)} custom-call(bf16[8,3,128,512]{3,2,1,0:T(8,128)(2,1)S(1)} %all-to-all-done.qkv_ref), custom_call_target="tpu_custom_call" | custom-call | flops 1073741824 | bytes 4194304 | tf_op jit(solution)/shard_map/pallas_call | solution.py:56
  92.4 29.7 %all_to_all.30.refs_0_ = bf16[8,128,512]{2,1,0:T(8,128)(2,1)S(1)} all-to-all(bf16[8,128,512]{2,1,0:T(8,128)(2,1)} %shard_map.96), channel_id=1, replica_groups=mesh['hi'=2,'lo'=4,'exp'=4] {'hi','lo'}, dimensions={0} | all-to-all | bytes 2097152 | tf_op jit(solution)/shard_map/all_to_all | solution.py:271
  122.1 2.0 shard_map.97
  125.9 45.2 %collective-permute-done.1 = bf16[128,4096]{1,0:T(8,128)(2,1)S(1)} collective-permute-done((bf16[128,4096]{1,0:T(8,128)(2,1)S(1)}, bf16[128,4096]{1,0:T(8,128)(2,1)S(1)}, u32[]{:S(2)}, u32[]{:S(2)}) %collective-permute-start.1) | collective-permute-done | bytes 1048608 | tf_op jit(solution)/shard_map/ppermute | solution.py:268
  171.1 2.2 convolution_convert_fusion
  173.3 3.7 %all-to-all-start.4 = ((bf16[16,16,4096]{2,1,0:T(8,128)(2,1)}), bf16[16,16,4096]{2,1,0:T(8,128)(2,1)S(1)}, u32[]{:S(2)}, u32[]{:S(2)}) async-start(bf16[16,16,4096]{2,1,0:T(8,128)(2,1)} %bitcast.34), calls=%async_computation.4 | async-start | bytes 4194304 | tf_op jit(solution)/shard_map/all_to_all | solution.py:271
  177.7 2.2 convolution_convert_fusion.1
  179.9 26.8 %all-to-all-done.4 = bf16[16,16,4096]{2,1,0:T(8,128)(2,1)S(1)} async-done(((bf16[16,16,4096]{2,1,0:T(8,128)(2,1)}), bf16[16,16,4096]{2,1,0:T(8,128)(2,1)S(1)}, u32[]{:S(2)}, u32[]{:S(2)}) %all-to-all-start.4) | async-done | bytes 2097184 | tf_op jit(solution)/shard_map/all_to_all | solution.py:271
  206.7 4.4 %all-to-all-start.2 = ((bf16[16,16,4096]{2,1,0:T(8,128)(2,1)}), bf16[16,16,4096]{2,1,0:T(8,128)(2,1)}, u32[]{:S(2)}, u32[]{:S(2)}) async-start(bf16[16,16,4096]{2,1,0:T(8,128)(2,1)} %bitcast.35), calls=%async_computation.2 | async-start | bytes 4194304 | tf_op jit(solution)/shard_map/all_to_all | solution.py:271
  211.1 9.4 %shard_map.99 = bf16[256,4096]{1,0:T(8,128)(2,1)S(1)} custom-call(bf16[256,4096]{1,0:T(8,128)(2,1)S(1)} %bitcast.28, bf16[1,4096,768]{2,1,0:T(8,128)(2,1)} %gate_hbm.3, bf16[1,4096,768]{2,1,0:T(8,128)(2,1)} %up_hbm.3, bf16[1,768,4096]{2,1,0:T(8,128)(2,1)} %down_hbm.3), custom_call_target="tpu_custom_call" | custom-call | flops 4831838208 | bytes 23068672 | tf_op jit(solution)/shard_map/pallas_call | solution.py:120
  220.5 1.3 copy-done
  221.8 19.0 %all-to-all-done.2 = bf16[16,16,4096]{2,1,0:T(8,128)(2,1)} async-done(((bf16[16,16,4096]{2,1,0:T(8,128)(2,1)}), bf16[16,16,4096]{2,1,0:T(8,128)(2,1)}, u32[]{:S(2)}, u32[]{:S(2)}) %all-to-all-start.2) | async-done | bytes 2097184 | tf_op jit(solution)/shard_map/all_to_all | solution.py:271
  240.8 3.9 %all-to-all-start.5 = ((bf16[16,16,4096]{2,1,0:T(8,128)(2,1)}), bf16[16,16,4096]{2,1,0:T(8,128)(2,1)S(1)}, u32[]{:S(2)}, u32[]{:S(2)}) async-start(bf16[16,16,4096]{2,1,0:T(8,128)(2,1)} %bitcast.29), calls=%async_computation.5 | async-start | bytes 4194304 | tf_op jit(solution)/shard_map/all_to_all | solution.py:271
  244.7 12.3 %shard_map.98 = bf16[256,4096]{1,0:T(8,128)(2,1)} custom-call(bf16[256,4096]{1,0:T(8,128)(2,1)} %bitcast.8.rows_ref, bf16[1,4096,768]{2,1,0:T(8,128)(2,1)} %gate_hbm.3, bf16[1,4096,768]{2,1,0:T(8,128)(2,1)} %up_hbm.3, bf16[1,768,4096]{2,1,0:T(8,128)(2,1)} %down_hbm.3), custom_call_target="tpu_custom_call" | custom-call | flops 4831838208 | bytes 23068672 | tf_op jit(solution)/shard_map/pallas_call | solution.py:120
  257.0 17.1 %all-to-all-done.5 = bf16[16,16,4096]{2,1,0:T(8,128)(2,1)S(1)} async-done(((bf16[16,16,4096]{2,1,0:T(8,128)(2,1)}), bf16[16,16,4096]{2,1,0:T(8,128)(2,1)S(1)}, u32[]{:S(2)}, u32[]{:S(2)}) %all-to-all-start.5) | async-done | bytes 2097184 | tf_op jit(solution)/shard_map/all_to_all | solution.py:271
  274.1 4.4 %all-to-all-start.3 = ((bf16[16,16,4096]{2,1,0:T(8,128)(2,1)}), bf16[16,16,4096]{2,1,0:T(8,128)(2,1)}, u32[]{:S(2)}, u32[]{:S(2)}) async-start(bf16[16,16,4096]{2,1,0:T(8,128)(2,1)} %bitcast.9), calls=%async_computation.3 | async-start | bytes 4194304 | tf_op jit(solution)/shard_map/all_to_all | solution.py:271
  280.1 1.6 collective-permute-start.2
  282.1 46.4 %all-to-all-done.3 = bf16[16,16,4096]{2,1,0:T(8,128)(2,1)} async-done(((bf16[16,16,4096]{2,1,0:T(8,128)(2,1)}), bf16[16,16,4096]{2,1,0:T(8,128)(2,1)}, u32[]{:S(2)}, u32[]{:S(2)}) %all-to-all-start.3) | async-done | bytes 2097184 | tf_op jit(solution)/shard_map/all_to_all | solution.py:271
  328.4 2.2 fusion.13
  330.7 3.5 %fusion.2 = bf16[1,128,4096]{2,1,0:T(8,128)(2,1)} fusion(bf16[128,4096]{1,0:T(8,128)(2,1)S(1)} %collective-permute-done.2, f32[128,4096]{1,0:T(8,128)S(1)} %fusion.13, bf16[256,4096]{1,0:T(8,128)(2,1)} %bitcast.10, bf16[128,4096]{1,0:T(8,128)(2,1)S(1)} %copy-done.3, f32[128]{0:T(128)S(1)} %get-tuple-element.13, s32[128]{0:T(128)S(1)} %get-tuple-element.15, ...), kind=kOutput, calls=%fused_computation.7 | convolution fusion | flops 271843328 | bytes 7342080 | tf_op jit(solution)/shard_map/dot_general | solution.py:251
  (35 shorter events, 4.7 us)
Async XLA Ops:
  3.5 7.3 %copy-start.4 = (s32[1,128,2]{1,2,0:T(2,128)S(1)}, s32[1,128,2]{1,2,0:T(2,128)}, u32[]{:S(2)}) copy-start(s32[1,128,2]{1,2,0:T(2,128)} %param.11) | copy-start | bytes 3076
  3.5 7.4 %copy-start.5 = (s32[1,128,2]{1,2,0:T(2,128)S(1)}, s32[1,128,2]{1,2,0:T(2,128)}, u32[]{:S(2)}) copy-start(s32[1,128,2]{1,2,0:T(2,128)} %param.12) | copy-start | bytes 3076
  3.5 80.8 %all-to-all-start = ((bf16[8,3,128,512]{3,2,1,0:T(8,128)(2,1)}), bf16[8,3,128,512]{3,2,1,0:T(8,128)(2,1)S(1)}, u32[]{:S(2)}, u32[]{:S(2)}) async-start(bf16[8,3,128,512]{3,2,1,0:T(8,128)(2,1)} %shard_map.95), calls=%async_computation | async-start | bytes 6291456 | tf_op jit(solution)/shard_map/all_to_all | solution.py:271
  11.1 73.2 %collective-permute-start = (s32[128,4]{1,0:T(8,128)S(1)}, s32[128,4]{1,0:T(8,128)S(1)}, u32[]{:S(2)}, u32[]{:S(2)}) collective-permute-start(s32[128,4]{1,0:T(8,128)S(1)} %pad_add_fusion), channel_id=1, source_target_pairs={{0,16},{4,20},{8,24},{12,28},{16,0},{20,4},{24,8},{28,12},{1,17},{... | collective-permute-start | bytes 6152 | tf_op jit(solution)/shard_map/ppermute | solution.py:268
  92.4 29.7 %copy-start.1 = (bf16[1,128,4096]{2,1,0:T(8,128)(2,1)S(1)}, bf16[1,128,4096]{2,1,0:T(8,128)(2,1)}, u32[]{:S(2)}) copy-start(bf16[1,128,4096]{2,1,0:T(8,128)(2,1)} %param.9) | copy-start | bytes 3145732
  92.4 29.7 %copy-start.2 = (f32[4096]{0:T(1024)S(1)}, f32[4096]{0:T(1024)}, u32[]{:S(2)}) copy-start(f32[4096]{0:T(1024)} %param.10) | copy-start | bytes 49156
  124.1 47.0 %collective-permute-start.1 = (bf16[128,4096]{1,0:T(8,128)(2,1)S(1)}, bf16[128,4096]{1,0:T(8,128)(2,1)S(1)}, u32[]{:S(2)}, u32[]{:S(2)}) collective-permute-start(bf16[128,4096]{1,0:T(8,128)(2,1)S(1)} %get-tuple-element.10), channel_id=1, source_target_pairs={{0,16},{4,20},{8,24},{12,28},{16,0},{20,4},{24,8},{28,12},{1,17},{... | collective-permute-start | bytes 3145736 | tf_op jit(solution)/shard_map/ppermute | solution.py:268
  173.3 33.4 %all-to-all-start.4 = ((bf16[16,16,4096]{2,1,0:T(8,128)(2,1)}), bf16[16,16,4096]{2,1,0:T(8,128)(2,1)S(1)}, u32[]{:S(2)}, u32[]{:S(2)}) async-start(bf16[16,16,4096]{2,1,0:T(8,128)(2,1)} %bitcast.34), calls=%async_computation.4 | async-start | bytes 4194304 | tf_op jit(solution)/shard_map/all_to_all | solution.py:271
  206.7 34.1 %all-to-all-start.2 = ((bf16[16,16,4096]{2,1,0:T(8,128)(2,1)}), bf16[16,16,4096]{2,1,0:T(8,128)(2,1)}, u32[]{:S(2)}, u32[]{:S(2)}) async-start(bf16[16,16,4096]{2,1,0:T(8,128)(2,1)} %bitcast.35), calls=%async_computation.2 | async-start | bytes 4194304 | tf_op jit(solution)/shard_map/all_to_all | solution.py:271
  220.5 1.3 copy-start
  240.8 33.4 %all-to-all-start.5 = ((bf16[16,16,4096]{2,1,0:T(8,128)(2,1)}), bf16[16,16,4096]{2,1,0:T(8,128)(2,1)S(1)}, u32[]{:S(2)}, u32[]{:S(2)}) async-start(bf16[16,16,4096]{2,1,0:T(8,128)(2,1)} %bitcast.29), calls=%async_computation.5 | async-start | bytes 4194304 | tf_op jit(solution)/shard_map/all_to_all | solution.py:271
  274.1 54.3 %all-to-all-start.3 = ((bf16[16,16,4096]{2,1,0:T(8,128)(2,1)}), bf16[16,16,4096]{2,1,0:T(8,128)(2,1)}, u32[]{:S(2)}, u32[]{:S(2)}) async-start(bf16[16,16,4096]{2,1,0:T(8,128)(2,1)} %bitcast.9), calls=%async_computation.3 | async-start | bytes 4194304 | tf_op jit(solution)/shard_map/all_to_all | solution.py:271
  280.1 50.5 %collective-permute-start.2 = (bf16[128,4096]{1,0:T(8,128)(2,1)S(1)}, bf16[128,4096]{1,0:T(8,128)(2,1)S(1)}, u32[]{:S(2)}, u32[]{:S(2)}) collective-permute-start(bf16[128,4096]{1,0:T(8,128)(2,1)S(1)} %fusion.1), channel_id=1, source_target_pairs={{0,16},{4,20},{8,24},{12,28},{16,0},{20,4},{24,8},{28,12},{1,17},{... | collective-permute-start | bytes 3145736 | tf_op jit(solution)/shard_map/ppermute | solution.py:268
  328.4 2.2 copy-start.3

commit v3 on v2

--- a/solution.py
+++ b/solution.py
@@ -68,44 +68,51 @@
     )(arrived)
 
 
-def expert_kernel(rows_ref, gate_hbm, up_hbm, down_hbm, out_ref, gate_ref, up_ref, down_ref, hidden_ref, arrived):
+def expert_kernel(rows_ref, gate_hbm, up_hbm, down_hbm, out_hbm, gate_ref, up_ref, down_ref, gate_total, up_total, out_ref, arrived, left):
     pieces = arrived.shape[1]
-    weights = ((gate_hbm, gate_ref), (up_hbm, up_ref), (down_hbm, down_ref))
-    copies = []
-    for kind, (source, target) in enumerate(weights):
+
+    def read(kind, source, target, piece):
         depth = target.shape[0] // pieces
-        group = []
-        for piece in range(pieces):
-            part = pl.ds(piece * depth, depth)
-            group.append(
-                pltpu.make_async_copy(source.at[0, part], target.at[part], arrived.at[kind, piece])
-            )
-        copies.append(group)
-    for copy in copies[0] + copies[1] + copies[2]:
+        part = pl.ds(piece * depth, depth)
+        return pltpu.make_async_copy(source.at[0, part], target.at[part], arrived.at[kind, piece])
+
+    gates = [read(0, gate_hbm, gate_ref, piece) for piece in range(pieces)]
+    ups = [read(1, up_hbm, up_ref, piece) for piece in range(pieces)]
+    downs = [read(2, down_hbm, down_ref, piece) for piece in range(pieces)]
+    for pair in zip(gates, ups):
+        for copy in pair:
+            copy.start()
+    for copy in downs:
         copy.start()
 
-    def columns_of(width, most):
-        tile = math.gcd(width, most)
-        return [slice(start, start + tile) for start in range(0, width, tile)]
-
-    rows = rows_ref[...]
-    for copy in copies[0]:
+    depth = gate_ref.shape[0] // pieces
+    for piece in range(pieces):
+        part = slice(piece * depth, (piece + 1) * depth)
+        for copy, weight, total in (
+            (gates[piece], gate_ref, gate_total),
+            (ups[piece], up_ref, up_total),
+        ):
+            copy.wait()
+            term = jnp.dot(rows_ref[:, part], weight[part], preferred_element_type=F32)
+            total[...] = total[...] + term if piece else term
+    gate = gate_total[...]
+    hidden = (gate / (1.0 + jnp.exp(-gate)) * up_total[...]).astype(BF)
+    for copy in downs:
         copy.wait()
-    gates = []
-    for columns in columns_of(gate_ref.shape[1], 256):
-        gates.append(jnp.dot(rows, gate_ref[:, columns], preferred_element_type=F32))
-    for copy in copies[1]:
-        copy.wait()
-    for gate, columns in zip(gates, columns_of(gate_ref.shape[1], 256)):
-        up = jnp.dot(rows, up_ref[:, columns], preferred_element_type=F32)
-        hidden_ref[:, columns] = (gate / (1.0 + jnp.exp(-gate)) * up).astype(BF)
-    hidden_rows = hidden_ref[...]
-    for copy in copies[2]:
-        copy.wait()
-    for columns in columns_of(down_ref.shape[1], 512):
+    width = out_ref.shape[1]
+    tile = width // left.shape[0]
+    writes = []
+    for index in range(left.shape[0]):
+        columns = slice(index * tile, (index + 1) * tile)
         out_ref[:, columns] = jnp.dot(
-            hidden_rows, down_ref[:, columns], preferred_element_type=F32
+            hidden, down_ref[:, columns], preferred_element_type=F32
         ).astype(BF)
+        columns = pl.ds(index * tile, tile)
+        write = pltpu.make_async_copy(out_ref.at[:, columns], out_hbm.at[:, columns], left.at[index])
+        write.start()
+        writes.append(write)
+    for write in writes:
+        write.wait()
 
 
 def in_hbm(array):
@@ -115,21 +122,24 @@
 def expert_ffn(rows, w_gate, w_up, w_down):
     count, width = rows.shape
     hidden = w_gate.shape[2]
-    vmem = pl.BlockSpec(memory_space=pltpu.VMEM)
     hbm = pl.BlockSpec(memory_space=pltpu.HBM)
+    pieces = math.gcd(width // 256, 4)
     return pl.pallas_call(
         expert_kernel,
-        in_specs=[vmem, hbm, hbm, hbm],
-        out_specs=vmem,
-        out_shape=jax.ShapeDtypeStruct((count, width), BF),
+        in_specs=[pl.BlockSpec(memory_space=pltpu.VMEM), hbm, hbm, hbm],
+        out_specs=hbm,
+        out_shape=pltpu.HBM((count, width), BF),
         scratch_shapes=[
             pltpu.VMEM((width, hidden), BF),
             pltpu.VMEM((width, hidden), BF),
             pltpu.VMEM((hidden, width), BF),
-            pltpu.VMEM((count, hidden), BF),
-            pltpu.SemaphoreType.DMA((3, 4)),
+            pltpu.VMEM((count, hidden), F32),
+            pltpu.VMEM((count, hidden), F32),
+            pltpu.VMEM((count, width), BF),
+            pltpu.SemaphoreType.DMA((3, pieces)),
+            pltpu.SemaphoreType.DMA((2 * pieces,)),
         ],
-        compiler_params=pltpu.CompilerParams(vmem_limit_bytes=30 << 20),
+        compiler_params=pltpu.CompilerParams(vmem_limit_bytes=32 << 20),
         cost_estimate=pl.CostEstimate(
             flops=6 * count * width * hidden,
             bytes_accessed=6 * width * hidden + 4 * count * width,
@@ -253,6 +263,33 @@
     )
 
 
+def finish_kernel(high_ref, low_ref, back_ref, stream_ref, other_ref, out_ref):
+    mixture = gather_back(high_ref[...], low_ref[...], back_ref[...])
+    total = stream_ref[...].astype(F32) + (mixture + other_ref[...].astype(F32))
+    out_ref[...] = total.astype(BF)
+
+
+def finish(high, low, back, stream, other):
+    rows, width = stream.shape
+    tile = math.gcd(width, 1024)
+    weight = pl.BlockSpec(high.shape, lambda step: (0, 0))
+    columns = pl.BlockSpec((rows, tile), lambda step: (0, step))
+    return pl.pallas_call(
+        finish_kernel,
+        grid=(width // tile,),
+        in_specs=[
+            weight,
+            weight,
+            pl.BlockSpec((back.shape[0], tile), lambda step: (0, step)),
+            columns,
+            columns,
+        ],
+        out_specs=columns,
+        out_shape=pltpu.HBM((rows, width), BF),
+        compiler_params=pltpu.CompilerParams(vmem_limit_bytes=16 << 20),
+    )(high, low, back, stream, other)
+
+
 def shards(projected, patches, norm_gain, expert_ids, gate_levels, w_gate, w_up, w_down):
     seq_count = lax.axis_size(SEQ)
     half_count = lax.axis_size(HALF)
@@ -261,7 +298,10 @@
     local_heads = HEADS // seq_count
     expert_count = 2 * half_count
     capacity = max(2, 4 * tok_rows // expert_count)
-    mirror = [(i, (i + lo_count) % seq_count) for i in range(seq_count)]
+    turned = [(i + lo_count // 2) % lo_count for i in range(lo_count)]
+    mirror = [
+        (i, (1 - i // lo_count) * lo_count + turned[i % lo_count]) for i in range(seq_count)
+    ]
     first = lax.axis_index("hi") * half_count
 
     def across(value):
@@ -277,12 +317,16 @@
     other = across(jnp.concatenate([expert_ids[0], gate_levels[0]], axis=1))
     outgoing = regroup(jnp.transpose(projected[0], (1, 0, 2)), seq_count)
     arrived = exchange(SEQ, outgoing)
-    arrived, other = lax.optimization_barrier((arrived, other))
     own_send, own_high, own_low = routing(
         expert_ids[0], gate_levels[0], first, half_count, capacity
     )
     other_send, other_high, other_low = routing(
         other[:, :2], other[:, 2:], first, half_count, capacity
+    )
+    arrived, own_send, own_high, own_low, other_send, other_high, other_low = (
+        lax.optimization_barrier(
+            (arrived, own_send, own_high, own_low, other_send, other_high, other_low)
+        )
     )
     returned = [exchange(SEQ, attention(arrived, local_heads))]
     attended, stream, normed = residual_norm(returned, patches[0], norm_gain[None], 1)
@@ -295,8 +339,7 @@
     other_back = routed(other_out)
     other_part = across(gather_back(other_high, other_low, other_back).astype(BF))
     own_back = routed(own_out)
-    own_total = stream.astype(F32) + gather_back(own_high, own_low, own_back)
-    layer_out = (own_total + other_part.astype(F32)).astype(BF)
+    layer_out = finish(own_high, own_low, own_back, stream, other_part)
     return (attended[None], layer_out[None])
 
 

time: 335 us -> 333 us (level)
  waiting for transfers between devices: 225 us -> 201 us
  starting transfers between devices: 29.4 us -> 51.6 us
    all_to_all x5, starting transfers between devices: 23.8 us -> 43.3 us  [exchange(): return lax.all_to_all(value, axes, split_axis=0, concat_axis=0, tiled=True)]
    ppermute x3, waiting for transfers between devices: 115 us -> 96.1 us  [across(): return lax.ppermute(value, SEQ, mirror)]
    all_to_all x5, waiting for transfers between devices: 109 us -> 104 us  [exchange(): return lax.all_to_all(value, axes, split_axis=0, concat_axis=0, tiled=True)]
    pallas_call x2 -> x3, Pallas kernels: 21.7 us -> 23.9 us  [the longest x2 19.9 us: expert_ffn(): pl.pallas_call(expert_kernel, in_specs=[pl.BlockSpec(memory_space=pltpu.V...]
  transfers between devices with their start and end apart: 8 -> 8, of which waited for: 6 -> 8; matrix products, arithmetic and copies ran while one was open for 2% -> 3% of each run, Pallas kernels for 6% -> 6%
where the time goes in v3:
time: 333 us
  waiting for transfers between devices  201 us (60%)
  starting transfers between devices  51.6 us (15%)
  Pallas kernels  36.9 us (11%)
  blocking collectives  31 us (9%)
  matrix products  7.75 us (2%)
    all_to_all x5, waiting for transfers between devices, exchange(): return lax.all_to_all(value, axes, split_axis=0, concat_axis=0, tiled=True)  104 us
    ppermute x3, waiting for transfers between devices, across(): return lax.ppermute(value, SEQ, mirror)  96.1 us
    all_to_all x5, starting transfers between devices, exchange(): return lax.all_to_all(value, axes, split_axis=0, concat_axis=0, tiled=True)  43.3 us
    all_to_all x1, blocking collectives, exchange(): return lax.all_to_all(value, axes, split_axis=0, concat_axis=0, tiled=True)  31 us
    pallas_call x2, Pallas kernels, expert_ffn(): pl.pallas_call(expert_kernel, in_specs=[pl.BlockSpec(memory_space=pltpu.V...  19.9 us
    ppermute x3, starting transfers between devices, across(): return lax.ppermute(value, SEQ, mirror)  8.38 us
    pallas_call x1, Pallas kernels, attention(): pl.pallas_call(functools.partial(attention_kernel, 2 * rows), grid=(local...  8.15 us
  transfers between devices with their start and end apart: 8, of which 8 were waited for; matrix products, arithmetic and copies ran while one was open for 3% of the time, Pallas kernels for 6%

profile of v3, /device:TPU:0, one launch (start us, length us, event | category | flops | bytes accessed | tf_op | source)
XLA Modules:
  0.0 332.8 jit_solution(9313670817099405151)
XLA Ops:
  0.6 2.8 shard_map.95
  3.5 7.3 %all-to-all-start = ((bf16[8,3,128,512]{3,2,1,0:T(8,128)(2,1)}), bf16[8,3,128,512]{3,2,1,0:T(8,128)(2,1)S(1)}, u32[]{:S(2)}, u32[]{:S(2)}) async-start(bf16[8,3,128,512]{3,2,1,0:T(8,128)(2,1)} %shard_map.95), calls=%async_computation | async-start | bytes 6291456 | tf_op jit(solution)/shard_map/all_to_all | solution.py:311
  11.1 3.9 %collective-permute-start = (s32[128,4]{1,0:T(8,128)S(1)}, s32[128,4]{1,0:T(8,128)S(1)}, u32[]{:S(2)}, u32[]{:S(2)}) collective-permute-start(s32[128,4]{1,0:T(8,128)S(1)} %pad_add_fusion), channel_id=1, source_target_pairs={{0,24},{4,28},{8,16},{12,20},{16,8},{20,12},{24,0},{28,4},{1,25},{... | collective-permute-start | bytes 6152 | tf_op jit(solution)/shard_map/ppermute | solution.py:308
  16.1 51.0 %collective-permute-done = s32[128,4]{1,0:T(8,128)S(1)} collective-permute-done((s32[128,4]{1,0:T(8,128)S(1)}, s32[128,4]{1,0:T(8,128)S(1)}, u32[]{:S(2)}, u32[]{:S(2)}) %collective-permute-start) | collective-permute-done | bytes 2080 | tf_op jit(solution)/shard_map/ppermute | solution.py:308
  68.6 15.0 %all-to-all-done.qkv_ref = bf16[8,3,128,512]{3,2,1,0:T(8,128)(2,1)S(1)} async-done(((bf16[8,3,128,512]{3,2,1,0:T(8,128)(2,1)}), bf16[8,3,128,512]{3,2,1,0:T(8,128)(2,1)S(1)}, u32[]{:S(2)}, u32[]{:S(2)}) %all-to-all-start) | async-done | bytes 3145760 | tf_op jit(solution)/shard_map/all_to_all | solution.py:311
  83.6 8.1 %shard_map.96 = bf16[8,128,512]{2,1,0:T(8,128)(2,1)} custom-call(bf16[8,3,128,512]{3,2,1,0:T(8,128)(2,1)S(1)} %all-to-all-done.qkv_ref), custom_call_target="tpu_custom_call" | custom-call | flops 1073741824 | bytes 4194304 | tf_op jit(solution)/shard_map/pallas_call | solution.py:56
  91.7 31.0 %all_to_all.30.refs_0_ = bf16[8,128,512]{2,1,0:T(8,128)(2,1)S(1)} all-to-all(bf16[8,128,512]{2,1,0:T(8,128)(2,1)} %shard_map.96), channel_id=1, replica_groups=mesh['hi'=2,'lo'=4,'exp'=4] {'hi','lo'}, dimensions={0} | all-to-all | bytes 2097152 | tf_op jit(solution)/shard_map/all_to_all | solution.py:311
  125.9 24.4 %collective-permute-done.1 = bf16[128,4096]{1,0:T(8,128)(2,1)S(1)} collective-permute-done((bf16[128,4096]{1,0:T(8,128)(2,1)S(1)}, bf16[128,4096]{1,0:T(8,128)(2,1)S(1)}, u32[]{:S(2)}, u32[]{:S(2)}) %collective-permute-start.1) | collective-permute-done | bytes 1048608 | tf_op jit(solution)/shard_map/ppermute | solution.py:308
  150.3 2.0 convolution_convert_fusion
  152.3 23.9 %all-to-all-start.4 = ((bf16[16,16,4096]{2,1,0:T(8,128)(2,1)}), bf16[16,16,4096]{2,1,0:T(8,128)(2,1)S(1)}, u32[]{:S(2)}, u32[]{:S(2)}) async-start(bf16[16,16,4096]{2,1,0:T(8,128)(2,1)} %bitcast.36), calls=%async_computation.4 | async-start | bytes 4194304 | tf_op jit(solution)/shard_map/all_to_all | solution.py:311
  176.2 2.1 convolution_convert_fusion.1
  178.3 27.6 %all-to-all-done.4 = bf16[16,16,4096]{2,1,0:T(8,128)(2,1)S(1)} async-done(((bf16[16,16,4096]{2,1,0:T(8,128)(2,1)}), bf16[16,16,4096]{2,1,0:T(8,128)(2,1)S(1)}, u32[]{:S(2)}, u32[]{:S(2)}) %all-to-all-start.4) | async-done | bytes 2097184 | tf_op jit(solution)/shard_map/all_to_all | solution.py:311
  205.9 4.4 %all-to-all-start.2 = ((bf16[16,16,4096]{2,1,0:T(8,128)(2,1)}), bf16[16,16,4096]{2,1,0:T(8,128)(2,1)}, u32[]{:S(2)}, u32[]{:S(2)}) async-start(bf16[16,16,4096]{2,1,0:T(8,128)(2,1)} %bitcast.35), calls=%async_computation.2 | async-start | bytes 4194304 | tf_op jit(solution)/shard_map/all_to_all | solution.py:311
  210.3 9.1 %shard_map.99 = bf16[256,4096]{1,0:T(8,128)(2,1)} custom-call(bf16[256,4096]{1,0:T(8,128)(2,1)S(1)} %bitcast.30, bf16[1,4096,768]{2,1,0:T(8,128)(2,1)} %gate_hbm.3, bf16[1,4096,768]{2,1,0:T(8,128)(2,1)} %up_hbm.3, bf16[1,768,4096]{2,1,0:T(8,128)(2,1)} %down_hbm.3), custom_call_target="tpu_custom_call" | custom-call | flops 4831838208 | bytes 23068672 | tf_op jit(solution)/shard_map/pallas_call | solution.py:127
  219.4 20.6 %all-to-all-done.2 = bf16[16,16,4096]{2,1,0:T(8,128)(2,1)} async-done(((bf16[16,16,4096]{2,1,0:T(8,128)(2,1)}), bf16[16,16,4096]{2,1,0:T(8,128)(2,1)}, u32[]{:S(2)}, u32[]{:S(2)}) %all-to-all-start.2) | async-done | bytes 2097184 | tf_op jit(solution)/shard_map/all_to_all | solution.py:311
  240.0 3.9 %all-to-all-start.5 = ((bf16[16,16,4096]{2,1,0:T(8,128)(2,1)}), bf16[16,16,4096]{2,1,0:T(8,128)(2,1)S(1)}, u32[]{:S(2)}, u32[]{:S(2)}) async-start(bf16[16,16,4096]{2,1,0:T(8,128)(2,1)} %bitcast.38), calls=%async_computation.5 | async-start | bytes 4194304 | tf_op jit(solution)/shard_map/all_to_all | solution.py:311
  243.9 10.7 %shard_map.98 = bf16[256,4096]{1,0:T(8,128)(2,1)} custom-call(bf16[256,4096]{1,0:T(8,128)(2,1)} %bitcast.8.rows_ref, bf16[1,4096,768]{2,1,0:T(8,128)(2,1)} %gate_hbm.3, bf16[1,4096,768]{2,1,0:T(8,128)(2,1)} %up_hbm.3, bf16[1,768,4096]{2,1,0:T(8,128)(2,1)} %down_hbm.3), custom_call_target="tpu_custom_call" | custom-call | flops 4831838208 | bytes 23068672 | tf_op jit(solution)/shard_map/pallas_call | solution.py:127
  254.6 18.7 %all-to-all-done.5 = bf16[16,16,4096]{2,1,0:T(8,128)(2,1)S(1)} async-done(((bf16[16,16,4096]{2,1,0:T(8,128)(2,1)}), bf16[16,16,4096]{2,1,0:T(8,128)(2,1)S(1)}, u32[]{:S(2)}, u32[]{:S(2)}) %all-to-all-start.5) | async-done | bytes 2097184 | tf_op jit(solution)/shard_map/all_to_all | solution.py:311
  274.6 3.7 %all-to-all-start.3 = ((bf16[16,16,4096]{2,1,0:T(8,128)(2,1)}), bf16[16,16,4096]{2,1,0:T(8,128)(2,1)S(1)}, u32[]{:S(2)}, u32[]{:S(2)}) async-start(bf16[16,16,4096]{2,1,0:T(8,128)(2,1)} %bitcast.37), calls=%async_computation.3 | async-start | bytes 4194304 | tf_op jit(solution)/shard_map/all_to_all | solution.py:311
  278.4 2.2 fusion.11
  282.0 3.3 collective-permute-start.2
  285.3 22.6 %all-to-all-done.3 = bf16[16,16,4096]{2,1,0:T(8,128)(2,1)S(1)} async-done(((bf16[16,16,4096]{2,1,0:T(8,128)(2,1)}), bf16[16,16,4096]{2,1,0:T(8,128)(2,1)S(1)}, u32[]{:S(2)}, u32[]{:S(2)}) %all-to-all-start.3) | async-done | bytes 2097184 | tf_op jit(solution)/shard_map/all_to_all | solution.py:311
  308.0 20.7 %collective-permute-done.2.other_ref = bf16[128,4096]{1,0:T(8,128)(2,1)} collective-permute-done((bf16[128,4096]{1,0:T(8,128)(2,1)}, bf16[128,4096]{1,0:T(8,128)(2,1)}, u32[]{:S(2)}, u32[]{:S(2)}) %collective-permute-start.2) | collective-permute-done | bytes 1048608 | tf_op jit(solution)/shard_map/ppermute | solution.py:308
  328.7 4.1 %shard_map.100 = bf16[128,4096]{1,0:T(8,128)(2,1)} custom-call(bf16[128,256]{1,0:T(8,128)(2,1)S(1)} %get-tuple-element.14.high_ref, bf16[128,256]{1,0:T(8,128)(2,1)S(1)} %get-tuple-element.15.low_ref, bf16[256,4096]{1,0:T(8,128)(2,1)S(1)} %bitcast.29, bf16[128,4096]{1,0:T(8,128)(2,1)S(1)} %copy-done.1, bf16[128,4096]{1,0:T(8,128)(2,1)} %collective-permute-done.2.other_ref), custom_call_target="tpu_custom_call" | custom-call | tf_op jit(solution)/shard_map/pallas_call | solution.py:277
  (38 shorter events, 8.8 us)
Async XLA Ops:
  3.5 7.3 %copy-start.5 = (s32[1,128,2]{1,2,0:T(2,128)S(1)}, s32[1,128,2]{1,2,0:T(2,128)}, u32[]{:S(2)}) copy-start(s32[1,128,2]{1,2,0:T(2,128)} %param.11) | copy-start | bytes 3076
  3.5 7.4 %copy-start.6 = (s32[1,128,2]{1,2,0:T(2,128)S(1)}, s32[1,128,2]{1,2,0:T(2,128)}, u32[]{:S(2)}) copy-start(s32[1,128,2]{1,2,0:T(2,128)} %param.12) | copy-start | bytes 3076
  3.5 80.1 %all-to-all-start = ((bf16[8,3,128,512]{3,2,1,0:T(8,128)(2,1)}), bf16[8,3,128,512]{3,2,1,0:T(8,128)(2,1)S(1)}, u32[]{:S(2)}, u32[]{:S(2)}) async-start(bf16[8,3,128,512]{3,2,1,0:T(8,128)(2,1)} %shard_map.95), calls=%async_computation | async-start | bytes 6291456 | tf_op jit(solution)/shard_map/all_to_all | solution.py:311
  11.1 56.0 %collective-permute-start = (s32[128,4]{1,0:T(8,128)S(1)}, s32[128,4]{1,0:T(8,128)S(1)}, u32[]{:S(2)}, u32[]{:S(2)}) collective-permute-start(s32[128,4]{1,0:T(8,128)S(1)} %pad_add_fusion), channel_id=1, source_target_pairs={{0,24},{4,28},{8,16},{12,20},{16,8},{20,12},{24,0},{28,4},{1,25},{... | collective-permute-start | bytes 6152 | tf_op jit(solution)/shard_map/ppermute | solution.py:308
  91.7 31.0 %copy-start = (bf16[1,128,4096]{2,1,0:T(8,128)(2,1)S(1)}, bf16[1,128,4096]{2,1,0:T(8,128)(2,1)}, u32[]{:S(2)}) copy-start(bf16[1,128,4096]{2,1,0:T(8,128)(2,1)} %param.9) | copy-start | bytes 3145732
  91.7 31.0 %copy-start.2 = (f32[4096]{0:T(1024)S(1)}, f32[4096]{0:T(1024)}, u32[]{:S(2)}) copy-start(f32[4096]{0:T(1024)} %param.10) | copy-start | bytes 49156
  124.7 25.5 %collective-permute-start.1 = (bf16[128,4096]{1,0:T(8,128)(2,1)S(1)}, bf16[128,4096]{1,0:T(8,128)(2,1)S(1)}, u32[]{:S(2)}, u32[]{:S(2)}) collective-permute-start(bf16[128,4096]{1,0:T(8,128)(2,1)S(1)} %get-tuple-element.17), channel_id=1, source_target_pairs={{0,24},{4,28},{8,16},{12,20},{16,8},{20,12},{24,0},{28,4},{1,25},{... | collective-permute-start | bytes 3145736 | tf_op jit(solution)/shard_map/ppermute | solution.py:308
  152.3 53.6 %all-to-all-start.4 = ((bf16[16,16,4096]{2,1,0:T(8,128)(2,1)}), bf16[16,16,4096]{2,1,0:T(8,128)(2,1)S(1)}, u32[]{:S(2)}, u32[]{:S(2)}) async-start(bf16[16,16,4096]{2,1,0:T(8,128)(2,1)} %bitcast.36), calls=%async_computation.4 | async-start | bytes 4194304 | tf_op jit(solution)/shard_map/all_to_all | solution.py:311
  205.9 34.1 %all-to-all-start.2 = ((bf16[16,16,4096]{2,1,0:T(8,128)(2,1)}), bf16[16,16,4096]{2,1,0:T(8,128)(2,1)}, u32[]{:S(2)}, u32[]{:S(2)}) async-start(bf16[16,16,4096]{2,1,0:T(8,128)(2,1)} %bitcast.35), calls=%async_computation.2 | async-start | bytes 4194304 | tf_op jit(solution)/shard_map/all_to_all | solution.py:311
  240.0 33.4 %all-to-all-start.5 = ((bf16[16,16,4096]{2,1,0:T(8,128)(2,1)}), bf16[16,16,4096]{2,1,0:T(8,128)(2,1)S(1)}, u32[]{:S(2)}, u32[]{:S(2)}) async-start(bf16[16,16,4096]{2,1,0:T(8,128)(2,1)} %bitcast.38), calls=%async_computation.5 | async-start | bytes 4194304 | tf_op jit(solution)/shard_map/all_to_all | solution.py:311
  273.3 1.3 copy-start.3
  274.6 33.4 %all-to-all-start.3 = ((bf16[16,16,4096]{2,1,0:T(8,128)(2,1)}), bf16[16,16,4096]{2,1,0:T(8,128)(2,1)S(1)}, u32[]{:S(2)}, u32[]{:S(2)}) async-start(bf16[16,16,4096]{2,1,0:T(8,128)(2,1)} %bitcast.37), calls=%async_computation.3 | async-start | bytes 4194304 | tf_op jit(solution)/shard_map/all_to_all | solution.py:311
  278.4 2.2 copy-start.4
  280.6 48.2 %copy-start.1 = (bf16[128,4096]{1,0:T(8,128)(2,1)S(1)}, bf16[128,4096]{1,0:T(8,128)(2,1)}, u32[]{:S(2)}) copy-start(bf16[128,4096]{1,0:T(8,128)(2,1)} %get-tuple-element.18.stream_ref) | copy-start | bytes 3145732
  282.0 46.7 %collective-permute-start.2 = (bf16[128,4096]{1,0:T(8,128)(2,1)}, bf16[128,4096]{1,0:T(8,128)(2,1)}, u32[]{:S(2)}, u32[]{:S(2)}) collective-permute-start(bf16[128,4096]{1,0:T(8,128)(2,1)} %fusion), channel_id=1, source_target_pairs={{0,24},{4,28},{8,16},{12,20},{16,8},{20,12},{24,0},{28,4},{1,25},{... | collective-permute-start | bytes 3145736 | tf_op jit(solution)/shard_map/ppermute | solution.py:308

commit v4 on v3

--- a/solution.py
+++ b/solution.py
@@ -23,27 +23,52 @@
     factor = math.log2(math.e) / math.sqrt(head_width)
     queries = qkv_ref[:, 0].reshape(length, head_width)
     keys = qkv_ref[:, 1].reshape(length, head_width)
-    values = qkv_ref[:, 2].reshape(length, head_width)
+    values = qkv_ref[:, 2].reshape(length, head_width).T
     over_width = (((1,), (1,)), ((), ()))
     shape = (step_rows, step_rows)
-    seen = lax.broadcasted_iota(jnp.int32, shape, 1) <= lax.broadcasted_iota(jnp.int32, shape, 0)
-    for start in range(0, length, step_rows):
-        stop = start + step_rows
+    seen = lax.broadcasted_iota(jnp.int32, shape, 0) <= lax.broadcasted_iota(jnp.int32, shape, 1)
+    half = step_rows // 2
+    starts = range(0, length, step_rows)
+    scores = []
+    for start in starts:
+        middle, stop = start + half, start + step_rows
         part = queries[start:stop]
-        near = lax.dot_general(part, keys[start:stop], over_width, preferred_element_type=F32)
-        near = jnp.where(seen, near, F32(-1e30))
-        highest = jnp.max(near, axis=-1, keepdims=True)
+        pieces = [
+            lax.dot_general(keys[start:middle], part, over_width, preferred_element_type=F32),
+            lax.dot_general(
+                keys[middle:stop], part[half:], over_width, preferred_element_type=F32
+            ),
+        ]
+        pieces[0] = jnp.where(seen[:half], pieces[0], F32(-1e30))
+        pieces[1] = jnp.where(seen[:half, :half], pieces[1], F32(-1e30))
         if start:
-            far = lax.dot_general(part, keys[:start], over_width, preferred_element_type=F32)
-            highest = jnp.maximum(highest, jnp.max(far, axis=-1, keepdims=True))
+            pieces.append(
+                lax.dot_general(keys[:start], part, over_width, preferred_element_type=F32)
+            )
+        scores.append(pieces)
+    for start, (near, last, *far) in zip(starts, scores):
+        middle, stop = start + half, start + step_rows
+        highest = jnp.max(near, axis=0, keepdims=True)
+        for piece in far:
+            highest = jnp.maximum(highest, jnp.max(piece, axis=0, keepdims=True))
+        high_last = jnp.maximum(highest[:, half:], jnp.max(last, axis=0, keepdims=True))
+        highest = jnp.concatenate([highest[:, :half], high_last], axis=1)
         near = jnp.exp2((near - highest) * factor)
-        total = jnp.sum(near, axis=-1, keepdims=True)
-        mixed = jnp.dot(near.astype(BF), values[start:stop], preferred_element_type=F32)
-        if start:
-            far = jnp.exp2((far - highest) * factor)
-            total += jnp.sum(far, axis=-1, keepdims=True)
-            mixed += jnp.dot(far.astype(BF), values[:start], preferred_element_type=F32)
-        mixed = (mixed / total).astype(BF)
+        total = jnp.sum(near, axis=0, keepdims=True)
+        mixed = jnp.dot(values[:, start:middle], near.astype(BF), preferred_element_type=F32)
+        for piece in far:
+            piece = jnp.exp2((piece - highest) * factor)
+            total += jnp.sum(piece, axis=0, keepdims=True)
+            mixed += jnp.dot(values[:, :start], piece.astype(BF), preferred_element_type=F32)
+        last = jnp.exp2((last - high_last) * factor)
+        total_last = total[:, half:] + jnp.sum(last, axis=0, keepdims=True)
+        mixed_last = mixed[:, half:] + jnp.dot(
+            values[:, middle:stop], last.astype(BF), preferred_element_type=F32
+        )
+        mixed = jnp.concatenate(
+            [mixed[:, :half] / total[:, :half], mixed_last / total_last], axis=1
+        )
+        mixed = mixed.T.astype(BF)
         for block in range(start // rows, stop // rows):
             low = block * rows - start
             out_ref[block] = mixed[low : low + rows]
@@ -54,7 +79,7 @@
     head_width = local_width // local_heads
     length = blocks * rows
     return pl.pallas_call(
-        functools.partial(attention_kernel, 2 * rows),
+        functools.partial(attention_kernel, 4 * rows),
         grid=(local_heads,),
         in_specs=[pl.BlockSpec((blocks, 3, rows, head_width), lambda head: (0, 0, 0, head))],
         out_specs=pl.BlockSpec((blocks, rows, head_width), lambda head: (0, 0, head)),
@@ -68,7 +93,7 @@
     )(arrived)
 
 
-def expert_kernel(rows_ref, gate_hbm, up_hbm, down_hbm, out_hbm, gate_ref, up_ref, down_ref, gate_total, up_total, out_ref, arrived, left):
+def expert_kernel(rows_hbm, gate_hbm, up_hbm, down_hbm, out_hbm, rows_ref, gate_ref, up_ref, down_ref, gate_total, up_total, out_ref, arrived, left):
     pieces = arrived.shape[1]
 
     def read(kind, source, target, piece):
@@ -79,15 +104,24 @@
     gates = [read(0, gate_hbm, gate_ref, piece) for piece in range(pieces)]
     ups = [read(1, up_hbm, up_ref, piece) for piece in range(pieces)]
     downs = [read(2, down_hbm, down_ref, piece) for piece in range(pieces)]
-    for pair in zip(gates, ups):
-        for copy in pair:
+    depth = gate_ref.shape[0] // pieces
+    rows = []
+    for piece in range(pieces):
+        part = pl.ds(piece * depth, depth)
+        rows.append(
+            pltpu.make_async_copy(
+                rows_hbm.at[:, part], rows_ref.at[:, part], arrived.at[3, piece]
+            )
+        )
+    for group in zip(rows, gates, ups):
+        for copy in group:
             copy.start()
     for copy in downs:
         copy.start()
 
-    depth = gate_ref.shape[0] // pieces
     for piece in range(pieces):
         part = slice(piece * depth, (piece + 1) * depth)
+        rows[piece].wait()
         for copy, weight, total in (
             (gates[piece], gate_ref, gate_total),
             (ups[piece], up_ref, up_total),
@@ -126,17 +160,18 @@
     pieces = math.gcd(width // 256, 4)
     return pl.pallas_call(
         expert_kernel,
-        in_specs=[pl.BlockSpec(memory_space=pltpu.VMEM), hbm, hbm, hbm],
+        in_specs=[pl.BlockSpec(memory_space=pl.ANY), hbm, hbm, hbm],
         out_specs=hbm,
         out_shape=pltpu.HBM((count, width), BF),
         scratch_shapes=[
+            pltpu.VMEM((count, width), BF),
             pltpu.VMEM((width, hidden), BF),
             pltpu.VMEM((width, hidden), BF),
             pltpu.VMEM((hidden, width), BF),
             pltpu.VMEM((count, hidden), F32),
             pltpu.VMEM((count, hidden), F32),
             pltpu.VMEM((count, width), BF),
-            pltpu.SemaphoreType.DMA((3, pieces)),
+            pltpu.SemaphoreType.DMA((4, pieces)),
             pltpu.SemaphoreType.DMA((2 * pieces,)),
         ],
         compiler_params=pltpu.CompilerParams(vmem_limit_bytes=32 << 20),
@@ -263,29 +298,34 @@
     )
 
 
-def finish_kernel(high_ref, low_ref, back_ref, stream_ref, other_ref, out_ref):
-    mixture = gather_back(high_ref[...], low_ref[...], back_ref[...])
-    total = stream_ref[...].astype(F32) + (mixture + other_ref[...].astype(F32))
-    out_ref[...] = total.astype(BF)
+def finish_kernel(high_ref, low_ref, back_ref, stream_ref, other_ref, out_hbm, out_ref, left):
+    tile = out_ref.shape[1] // left.shape[0]
+    writes = []
+    for index in range(left.shape[0]):
+        columns = slice(index * tile, (index + 1) * tile)
+        mixture = gather_back(high_ref[...], low_ref[...], back_ref[:, columns])
+        mixture = mixture + other_ref[:, columns].astype(F32)
+        out_ref[:, columns] = (stream_ref[:, columns].astype(F32) + mixture).astype(BF)
+        columns = pl.ds(index * tile, tile)
+        write = pltpu.make_async_copy(out_ref.at[:, columns], out_hbm.at[:, columns], left.at[index])
+        write.start()
+        writes.append(write)
+    for write in writes:
+        write.wait()
 
 
 def finish(high, low, back, stream, other):
     rows, width = stream.shape
-    tile = math.gcd(width, 1024)
-    weight = pl.BlockSpec(high.shape, lambda step: (0, 0))
-    columns = pl.BlockSpec((rows, tile), lambda step: (0, step))
+    vmem = pl.BlockSpec(memory_space=pltpu.VMEM)
     return pl.pallas_call(
         finish_kernel,
-        grid=(width // tile,),
-        in_specs=[
-            weight,
-            weight,
-            pl.BlockSpec((back.shape[0], tile), lambda step: (0, step)),
-            columns,
-            columns,
+        in_specs=[vmem] * 5,
+        out_specs=pl.BlockSpec(memory_space=pltpu.HBM),
+        out_shape=pltpu.HBM((rows, width), BF),
+        scratch_shapes=[
+            pltpu.VMEM((rows, width), BF),
+            pltpu.SemaphoreType.DMA((math.gcd(width // 256, 4),)),
         ],
-        out_specs=columns,
-        out_shape=pltpu.HBM((rows, width), BF),
         compiler_params=pltpu.CompilerParams(vmem_limit_bytes=16 << 20),
     )(high, low, back, stream, other)
 

time: 333 us -> 330 us (level)
  Pallas kernels: 36.9 us -> 32.1 us
    pallas_call x4, Pallas kernels: 32.1 us -> 27.4 us  [the longest x2 19 us: expert_ffn(): pl.pallas_call(expert_kernel, in_specs=[pl.BlockSpec(memory_space=pl.ANY)...]
where the time goes in v4:
time: 330 us; the launch traced here: 329 us
  waiting for transfers between devices  201 us (61%)
  starting transfers between devices  51.6 us (16%)
  Pallas kernels  32.1 us (10%)
  blocking collectives  31 us (9%)
  matrix products  7.74 us (2%)
    all_to_all x5, waiting for transfers between devices, exchange(): return lax.all_to_all(value, axes, split_axis=0, concat_axis=0, tiled=True)  105 us
    ppermute x3, waiting for transfers between devices, across(): return lax.ppermute(value, SEQ, mirror)  96.2 us
    all_to_all x5, starting transfers between devices, exchange(): return lax.all_to_all(value, axes, split_axis=0, concat_axis=0, tiled=True)  43.3 us
    all_to_all x1, blocking collectives, exchange(): return lax.all_to_all(value, axes, split_axis=0, concat_axis=0, tiled=True)  31 us
    pallas_call x2, Pallas kernels, expert_ffn(): pl.pallas_call(expert_kernel, in_specs=[pl.BlockSpec(memory_space=pl.ANY)...  19 us
    ppermute x3, starting transfers between devices, across(): return lax.ppermute(value, SEQ, mirror)  8.38 us
  transfers between devices with their start and end apart: 8, of which 8 were waited for; matrix products, arithmetic and copies ran while one was open for 3% of the time, Pallas kernels for 6%

profile of v4, /device:TPU:0, one launch (start us, length us, event | category | flops | bytes accessed | tf_op | source)
XLA Modules:
  0.0 329.1 jit_solution(16414324762804456178)
XLA Ops:
  0.6 2.8 shard_map.95
  3.5 7.3 %all-to-all-start = ((bf16[8,3,128,512]{3,2,1,0:T(8,128)(2,1)}), bf16[8,3,128,512]{3,2,1,0:T(8,128)(2,1)S(1)}, u32[]{:S(2)}, u32[]{:S(2)}) async-start(bf16[8,3,128,512]{3,2,1,0:T(8,128)(2,1)} %shard_map.95), calls=%async_computation | async-start | bytes 6291456 | tf_op jit(solution)/shard_map/all_to_all | solution.py:351
  11.1 3.9 %collective-permute-start = (s32[128,4]{1,0:T(8,128)S(1)}, s32[128,4]{1,0:T(8,128)S(1)}, u32[]{:S(2)}, u32[]{:S(2)}) collective-permute-start(s32[128,4]{1,0:T(8,128)S(1)} %pad_add_fusion), channel_id=1, source_target_pairs={{0,24},{4,28},{8,16},{12,20},{16,8},{20,12},{24,0},{28,4},{1,25},{... | collective-permute-start | bytes 6152 | tf_op jit(solution)/shard_map/ppermute | solution.py:348
  16.1 51.0 %collective-permute-done = s32[128,4]{1,0:T(8,128)S(1)} collective-permute-done((s32[128,4]{1,0:T(8,128)S(1)}, s32[128,4]{1,0:T(8,128)S(1)}, u32[]{:S(2)}, u32[]{:S(2)}) %collective-permute-start) | collective-permute-done | bytes 2080 | tf_op jit(solution)/shard_map/ppermute | solution.py:348
  68.6 15.0 %all-to-all-done.qkv_ref = bf16[8,3,128,512]{3,2,1,0:T(8,128)(2,1)S(1)} async-done(((bf16[8,3,128,512]{3,2,1,0:T(8,128)(2,1)}), bf16[8,3,128,512]{3,2,1,0:T(8,128)(2,1)S(1)}, u32[]{:S(2)}, u32[]{:S(2)}) %all-to-all-start) | async-done | bytes 3145760 | tf_op jit(solution)/shard_map/all_to_all | solution.py:351
  83.6 5.6 %shard_map.96 = bf16[8,128,512]{2,1,0:T(8,128)(2,1)} custom-call(bf16[8,3,128,512]{3,2,1,0:T(8,128)(2,1)S(1)} %all-to-all-done.qkv_ref), custom_call_target="tpu_custom_call" | custom-call | flops 1073741824 | bytes 4194304 | tf_op jit(solution)/shard_map/pallas_call | solution.py:81
  89.2 31.0 %all_to_all.30.refs_0_ = bf16[8,128,512]{2,1,0:T(8,128)(2,1)S(1)} all-to-all(bf16[8,128,512]{2,1,0:T(8,128)(2,1)} %shard_map.96), channel_id=1, replica_groups=mesh['hi'=2,'lo'=4,'exp'=4] {'hi','lo'}, dimensions={0} | all-to-all | bytes 2097152 | tf_op jit(solution)/shard_map/all_to_all | solution.py:351
  123.4 24.4 %collective-permute-done.1 = bf16[128,4096]{1,0:T(8,128)(2,1)S(1)} collective-permute-done((bf16[128,4096]{1,0:T(8,128)(2,1)S(1)}, bf16[128,4096]{1,0:T(8,128)(2,1)S(1)}, u32[]{:S(2)}, u32[]{:S(2)}) %collective-permute-start.1) | collective-permute-done | bytes 1048608 | tf_op jit(solution)/shard_map/ppermute | solution.py:348
  147.7 2.0 convolution_convert_fusion
  149.8 23.9 %all-to-all-start.4 = ((bf16[16,16,4096]{2,1,0:T(8,128)(2,1)}), bf16[16,16,4096]{2,1,0:T(8,128)(2,1)S(1)}, u32[]{:S(2)}, u32[]{:S(2)}) async-start(bf16[16,16,4096]{2,1,0:T(8,128)(2,1)} %bitcast.36), calls=%async_computation.4 | async-start | bytes 4194304 | tf_op jit(solution)/shard_map/all_to_all | solution.py:351
  173.7 2.1 convolution_convert_fusion.1
  175.7 27.6 %all-to-all-done.4 = bf16[16,16,4096]{2,1,0:T(8,128)(2,1)S(1)} async-done(((bf16[16,16,4096]{2,1,0:T(8,128)(2,1)}), bf16[16,16,4096]{2,1,0:T(8,128)(2,1)S(1)}, u32[]{:S(2)}, u32[]{:S(2)}) %all-to-all-start.4) | async-done | bytes 2097184 | tf_op jit(solution)/shard_map/all_to_all | solution.py:351
  203.3 4.4 %all-to-all-start.2 = ((bf16[16,16,4096]{2,1,0:T(8,128)(2,1)}), bf16[16,16,4096]{2,1,0:T(8,128)(2,1)}, u32[]{:S(2)}, u32[]{:S(2)}) async-start(bf16[16,16,4096]{2,1,0:T(8,128)(2,1)} %bitcast.35), calls=%async_computation.2 | async-start | bytes 4194304 | tf_op jit(solution)/shard_map/all_to_all | solution.py:351
  207.8 9.2 %shard_map.99 = bf16[256,4096]{1,0:T(8,128)(2,1)} custom-call(bf16[256,4096]{1,0:T(8,128)(2,1)S(1)} %bitcast.30, bf16[1,4096,768]{2,1,0:T(8,128)(2,1)} %gate_hbm.3, bf16[1,4096,768]{2,1,0:T(8,128)(2,1)} %up_hbm.3, bf16[1,768,4096]{2,1,0:T(8,128)(2,1)} %down_hbm.3), custom_call_target="tpu_custom_call" | custom-call | flops 4831838208 | bytes 23068672 | tf_op jit(solution)/shard_map/pallas_call | solution.py:161
  217.0 20.5 %all-to-all-done.2 = bf16[16,16,4096]{2,1,0:T(8,128)(2,1)} async-done(((bf16[16,16,4096]{2,1,0:T(8,128)(2,1)}), bf16[16,16,4096]{2,1,0:T(8,128)(2,1)}, u32[]{:S(2)}, u32[]{:S(2)}) %all-to-all-start.2) | async-done | bytes 2097184 | tf_op jit(solution)/shard_map/all_to_all | solution.py:351
  237.4 3.9 %all-to-all-start.5 = ((bf16[16,16,4096]{2,1,0:T(8,128)(2,1)}), bf16[16,16,4096]{2,1,0:T(8,128)(2,1)S(1)}, u32[]{:S(2)}, u32[]{:S(2)}) async-start(bf16[16,16,4096]{2,1,0:T(8,128)(2,1)} %bitcast.38), calls=%async_computation.5 | async-start | bytes 4194304 | tf_op jit(solution)/shard_map/all_to_all | solution.py:351
  241.3 9.8 %shard_map.98 = bf16[256,4096]{1,0:T(8,128)(2,1)} custom-call(bf16[256,4096]{1,0:T(8,128)(2,1)} %bitcast.8.rows_hbm, bf16[1,4096,768]{2,1,0:T(8,128)(2,1)} %gate_hbm.3, bf16[1,4096,768]{2,1,0:T(8,128)(2,1)} %up_hbm.3, bf16[1,768,4096]{2,1,0:T(8,128)(2,1)} %down_hbm.3), custom_call_target="tpu_custom_call" | custom-call | flops 4831838208 | bytes 23068672 | tf_op jit(solution)/shard_map/pallas_call | solution.py:161
  251.2 19.6 %all-to-all-done.5 = bf16[16,16,4096]{2,1,0:T(8,128)(2,1)S(1)} async-done(((bf16[16,16,4096]{2,1,0:T(8,128)(2,1)}), bf16[16,16,4096]{2,1,0:T(8,128)(2,1)S(1)}, u32[]{:S(2)}, u32[]{:S(2)}) %all-to-all-start.5) | async-done | bytes 2097184 | tf_op jit(solution)/shard_map/all_to_all | solution.py:351
  272.1 3.7 %all-to-all-start.3 = ((bf16[16,16,4096]{2,1,0:T(8,128)(2,1)}), bf16[16,16,4096]{2,1,0:T(8,128)(2,1)S(1)}, u32[]{:S(2)}, u32[]{:S(2)}) async-start(bf16[16,16,4096]{2,1,0:T(8,128)(2,1)} %bitcast.37), calls=%async_computation.3 | async-start | bytes 4194304 | tf_op jit(solution)/shard_map/all_to_all | solution.py:351
  275.8 2.2 fusion.11
  279.5 3.3 %collective-permute-start.2 = (bf16[128,4096]{1,0:T(8,128)(2,1)}, bf16[128,4096]{1,0:T(8,128)(2,1)}, u32[]{:S(2)}, u32[]{:S(2)}) collective-permute-start(bf16[128,4096]{1,0:T(8,128)(2,1)} %fusion), channel_id=1, source_target_pairs={{0,24},{4,28},{8,16},{12,20},{16,8},{20,12},{24,0},{28,4},{1,25},{... | collective-permute-start | bytes 3145736 | tf_op jit(solution)/shard_map/ppermute | solution.py:348
  282.8 22.6 %all-to-all-done.3 = bf16[16,16,4096]{2,1,0:T(8,128)(2,1)S(1)} async-done(((bf16[16,16,4096]{2,1,0:T(8,128)(2,1)}), bf16[16,16,4096]{2,1,0:T(8,128)(2,1)S(1)}, u32[]{:S(2)}, u32[]{:S(2)}) %all-to-all-start.3) | async-done | bytes 2097184 | tf_op jit(solution)/shard_map/all_to_all | solution.py:351
  305.4 20.8 %collective-permute-done.2.other_ref = bf16[128,4096]{1,0:T(8,128)(2,1)} collective-permute-done((bf16[128,4096]{1,0:T(8,128)(2,1)}, bf16[128,4096]{1,0:T(8,128)(2,1)}, u32[]{:S(2)}, u32[]{:S(2)}) %collective-permute-start.2) | collective-permute-done | bytes 1048608 | tf_op jit(solution)/shard_map/ppermute | solution.py:348
  326.2 2.7 shard_map.100
  (38 shorter events, 8.8 us)
Async XLA Ops:
  3.5 7.3 %copy-start.5 = (s32[1,128,2]{1,2,0:T(2,128)S(1)}, s32[1,128,2]{1,2,0:T(2,128)}, u32[]{:S(2)}) copy-start(s32[1,128,2]{1,2,0:T(2,128)} %param.11) | copy-start | bytes 3076
  3.5 7.4 %copy-start.6 = (s32[1,128,2]{1,2,0:T(2,128)S(1)}, s32[1,128,2]{1,2,0:T(2,128)}, u32[]{:S(2)}) copy-start(s32[1,128,2]{1,2,0:T(2,128)} %param.12) | copy-start | bytes 3076
  3.5 80.1 %all-to-all-start = ((bf16[8,3,128,512]{3,2,1,0:T(8,128)(2,1)}), bf16[8,3,128,512]{3,2,1,0:T(8,128)(2,1)S(1)}, u32[]{:S(2)}, u32[]{:S(2)}) async-start(bf16[8,3,128,512]{3,2,1,0:T(8,128)(2,1)} %shard_map.95), calls=%async_computation | async-start | bytes 6291456 | tf_op jit(solution)/shard_map/all_to_all | solution.py:351
  11.1 56.0 %collective-permute-start = (s32[128,4]{1,0:T(8,128)S(1)}, s32[128,4]{1,0:T(8,128)S(1)}, u32[]{:S(2)}, u32[]{:S(2)}) collective-permute-start(s32[128,4]{1,0:T(8,128)S(1)} %pad_add_fusion), channel_id=1, source_target_pairs={{0,24},{4,28},{8,16},{12,20},{16,8},{20,12},{24,0},{28,4},{1,25},{... | collective-permute-start | bytes 6152 | tf_op jit(solution)/shard_map/ppermute | solution.py:348
  89.2 31.0 %copy-start = (bf16[1,128,4096]{2,1,0:T(8,128)(2,1)S(1)}, bf16[1,128,4096]{2,1,0:T(8,128)(2,1)}, u32[]{:S(2)}) copy-start(bf16[1,128,4096]{2,1,0:T(8,128)(2,1)} %param.9) | copy-start | bytes 3145732
  89.2 31.0 %copy-start.2 = (f32[4096]{0:T(1024)S(1)}, f32[4096]{0:T(1024)}, u32[]{:S(2)}) copy-start(f32[4096]{0:T(1024)} %param.10) | copy-start | bytes 49156
  122.2 25.5 %collective-permute-start.1 = (bf16[128,4096]{1,0:T(8,128)(2,1)S(1)}, bf16[128,4096]{1,0:T(8,128)(2,1)S(1)}, u32[]{:S(2)}, u32[]{:S(2)}) collective-permute-start(bf16[128,4096]{1,0:T(8,128)(2,1)S(1)} %get-tuple-element.17), channel_id=1, source_target_pairs={{0,24},{4,28},{8,16},{12,20},{16,8},{20,12},{24,0},{28,4},{1,25},{... | collective-permute-start | bytes 3145736 | tf_op jit(solution)/shard_map/ppermute | solution.py:348
  149.8 53.6 %all-to-all-start.4 = ((bf16[16,16,4096]{2,1,0:T(8,128)(2,1)}), bf16[16,16,4096]{2,1,0:T(8,128)(2,1)S(1)}, u32[]{:S(2)}, u32[]{:S(2)}) async-start(bf16[16,16,4096]{2,1,0:T(8,128)(2,1)} %bitcast.36), calls=%async_computation.4 | async-start | bytes 4194304 | tf_op jit(solution)/shard_map/all_to_all | solution.py:351
  203.3 34.1 %all-to-all-start.2 = ((bf16[16,16,4096]{2,1,0:T(8,128)(2,1)}), bf16[16,16,4096]{2,1,0:T(8,128)(2,1)}, u32[]{:S(2)}, u32[]{:S(2)}) async-start(bf16[16,16,4096]{2,1,0:T(8,128)(2,1)} %bitcast.35), calls=%async_computation.2 | async-start | bytes 4194304 | tf_op jit(solution)/shard_map/all_to_all | solution.py:351
  237.4 33.4 %all-to-all-start.5 = ((bf16[16,16,4096]{2,1,0:T(8,128)(2,1)}), bf16[16,16,4096]{2,1,0:T(8,128)(2,1)S(1)}, u32[]{:S(2)}, u32[]{:S(2)}) async-start(bf16[16,16,4096]{2,1,0:T(8,128)(2,1)} %bitcast.38), calls=%async_computation.5 | async-start | bytes 4194304 | tf_op jit(solution)/shard_map/all_to_all | solution.py:351
  270.8 1.3 copy-start.3
  272.1 33.4 %all-to-all-start.3 = ((bf16[16,16,4096]{2,1,0:T(8,128)(2,1)}), bf16[16,16,4096]{2,1,0:T(8,128)(2,1)S(1)}, u32[]{:S(2)}, u32[]{:S(2)}) async-start(bf16[16,16,4096]{2,1,0:T(8,128)(2,1)} %bitcast.37), calls=%async_computation.3 | async-start | bytes 4194304 | tf_op jit(solution)/shard_map/all_to_all | solution.py:351
  275.8 2.2 copy-start.4
  278.0 48.2 %copy-start.1 = (bf16[128,4096]{1,0:T(8,128)(2,1)S(1)}, bf16[128,4096]{1,0:T(8,128)(2,1)}, u32[]{:S(2)}) copy-start(bf16[128,4096]{1,0:T(8,128)(2,1)} %get-tuple-element.18.stream_ref) | copy-start | bytes 3145732
  279.5 46.7 %collective-permute-start.2 = (bf16[128,4096]{1,0:T(8,128)(2,1)}, bf16[128,4096]{1,0:T(8,128)(2,1)}, u32[]{:S(2)}, u32[]{:S(2)}) collective-permute-start(bf16[128,4096]{1,0:T(8,128)(2,1)} %fusion), channel_id=1, source_target_pairs={{0,24},{4,28},{8,16},{12,20},{16,8},{20,12},{24,0},{28,4},{1,25},{... | collective-permute-start | bytes 3145736 | tf_op jit(solution)/shard_map/ppermute | solution.py:348

commit v5 on v4

--- a/solution.py
+++ b/solution.py
@@ -17,8 +17,16 @@
 F32 = jnp.float32
 
 
-def attention_kernel(step_rows, qkv_ref, out_ref):
+def turns(count):
+    return [*range(count - 2, 0, -1), count - 1]
+
+
+def attention_kernel(step_rows, me_ref, *refs):
+    *refs, qkv_ref, mixed_ref = refs
     blocks, _, rows, head_width = qkv_ref.shape
+    pieces, out_refs = refs[:blocks], refs[blocks:]
+    for turn, piece in enumerate(pieces):
+        qkv_ref[jnp.bitwise_xor(me_ref[0], turn)] = piece[...]
     length = blocks * rows
     factor = math.log2(math.e) / math.sqrt(head_width)
     queries = qkv_ref[:, 0].reshape(length, head_width)
@@ -71,26 +79,34 @@
         mixed = mixed.T.astype(BF)
         for block in range(start // rows, stop // rows):
             low = block * rows - start
-            out_ref[block] = mixed[low : low + rows]
-
-
-def attention(arrived, local_heads):
-    blocks, _, rows, local_width = arrived.shape
+            mixed_ref[block] = mixed[low : low + rows]
+    for turn, out_ref in enumerate(out_refs):
+        out_ref[...] = mixed_ref[jnp.bitwise_xor(me_ref[0], turn)]
+
+
+def attention(me, pieces, local_heads):
+    blocks = len(pieces)
+    _, rows, local_width = pieces[0].shape
     head_width = local_width // local_heads
     length = blocks * rows
+    piece = pl.BlockSpec((3, rows, head_width), lambda head: (0, 0, head))
     return pl.pallas_call(
         functools.partial(attention_kernel, 4 * rows),
         grid=(local_heads,),
-        in_specs=[pl.BlockSpec((blocks, 3, rows, head_width), lambda head: (0, 0, 0, head))],
-        out_specs=pl.BlockSpec((blocks, rows, head_width), lambda head: (0, 0, head)),
-        out_shape=pltpu.HBM((blocks, rows, local_width), BF),
+        in_specs=[pl.BlockSpec(memory_space=pltpu.SMEM)] + [piece] * blocks,
+        out_specs=[pl.BlockSpec((rows, head_width), lambda head: (0, head))] * blocks,
+        out_shape=[pltpu.HBM((rows, local_width), BF)] * blocks,
+        scratch_shapes=[
+            pltpu.VMEM((blocks, 3, rows, head_width), BF),
+            pltpu.VMEM((blocks, rows, head_width), BF),
+        ],
         compiler_params=pltpu.CompilerParams(vmem_limit_bytes=20 << 20),
         cost_estimate=pl.CostEstimate(
             flops=2 * length * length * local_width,
             bytes_accessed=8 * length * local_width,
             transcendentals=length * length * local_heads // 2,
         ),
-    )(arrived)
+    )(me, *pieces)
 
 
 def expert_kernel(rows_hbm, gate_hbm, up_hbm, down_hbm, out_hbm, rows_ref, gate_ref, up_ref, down_ref, gate_total, up_total, out_ref, arrived, left):
@@ -183,15 +199,17 @@
     )(rows, in_hbm(w_gate), in_hbm(w_up), in_hbm(w_down))
 
 
-def regroup_kernel(in_ref, out_ref, held, arrived, left):
-    blocks, _, _, local_width = held.shape
+def regroup_kernel(me_ref, in_ref, *refs):
+    *out_refs, held, arrived, left = refs
+    _, _, _, local_width = held.shape
     reads, writes = [], []
-    for block in range(blocks):
-        columns = pl.ds(block * local_width, local_width)
+    for turn, out_ref in enumerate(out_refs):
+        block = jnp.bitwise_xor(me_ref[0], turn)
+        columns = pl.ds(pl.multiple_of(block * local_width, local_width), local_width)
         reads.append(
-            pltpu.make_async_copy(in_ref.at[:, :, columns], held.at[block], arrived.at[block])
+            pltpu.make_async_copy(in_ref.at[:, :, columns], held.at[turn], arrived.at[turn])
         )
-        writes.append(pltpu.make_async_copy(held.at[block], out_ref.at[block], left.at[block]))
+        writes.append(pltpu.make_async_copy(held.at[turn], out_ref, left.at[turn]))
     for read in reads:
         read.start()
     for read, write in zip(reads, writes):
@@ -201,67 +219,56 @@
         write.wait()
 
 
-def regroup(projected, blocks):
+def regroup(me, projected, blocks):
     kinds, rows, width = projected.shape
-    shape = (blocks, kinds, rows, width // blocks)
+    shape = (kinds, rows, width // blocks)
     hbm = pl.BlockSpec(memory_space=pltpu.HBM)
     return pl.pallas_call(
         regroup_kernel,
-        in_specs=[hbm],
-        out_specs=hbm,
-        out_shape=pltpu.HBM(shape, BF),
+        in_specs=[pl.BlockSpec(memory_space=pltpu.SMEM), hbm],
+        out_specs=[hbm] * blocks,
+        out_shape=[pltpu.HBM(shape, BF)] * blocks,
         scratch_shapes=[
-            pltpu.VMEM(shape, BF),
+            pltpu.VMEM((blocks,) + shape, BF),
             pltpu.SemaphoreType.DMA((blocks,)),
             pltpu.SemaphoreType.DMA((blocks,)),
         ],
         compiler_params=pltpu.CompilerParams(vmem_limit_bytes=59 << 20),
-    )(projected)
-
-
-def norm_kernel(parts, *refs):
-    returned, (patches_ref, gain_ref, attended_ref, stream_ref) = refs[:parts], refs[parts:parts + 4]
-    normed_refs = refs[parts + 4 :]
-    blocks, _, part_width = returned[0].shape
+    )(me, projected)
+
+
+def norm_kernel(me_ref, *refs):
+    *pieces, patches_ref, gain_ref, attended_ref, stream_ref, normed_ref = refs
+    part_width = pieces[0].shape[1]
     total = 0.0
-    for block in range(blocks * parts):
-        columns = slice(block * part_width, (block + 1) * part_width)
-        part = returned[block % parts][block // parts]
+    for turn, piece in enumerate(pieces):
+        block = jnp.bitwise_xor(me_ref[0], turn)
+        columns = pl.ds(pl.multiple_of(block * part_width, part_width), part_width)
+        part = piece[...]
         attended_ref[:, columns] = part
         stream = (patches_ref[:, columns].astype(F32) + part.astype(F32)).astype(BF)
         stream_ref[:, columns] = stream
         stream_f = stream.astype(F32)
         total += jnp.sum(stream_f * stream_f, axis=-1, keepdims=True)
-    factor = lax.rsqrt(total / (blocks * parts * part_width) + 1e-05)
-    start = 0
-    for normed_ref in normed_refs:
-        stop = start + normed_ref.shape[1]
-        stream_f = stream_ref[:, start:stop].astype(F32)
-        normed_ref[...] = (stream_f * factor * gain_ref[:, start:stop]).astype(BF)
-        start = stop
-
-
-def residual_norm(returned, patches, gain, chunks):
-    blocks, rows, part_width = returned[0].shape
-    width = patches.shape[1]
+    factor = lax.rsqrt(total / stream_ref.shape[1] + 1e-05)
+    normed_ref[...] = (stream_ref[...].astype(F32) * factor * gain_ref[...]).astype(BF)
+
+
+def residual_norm(me, pieces, patches, gain):
+    rows, width = patches.shape
     tile = math.gcd(rows, 32)
     at = lambda step: (step, 0)
-    shape = lambda columns: jax.ShapeDtypeStruct((rows, columns), BF)
+    whole = pl.BlockSpec((tile, width), at)
     return pl.pallas_call(
-        functools.partial(norm_kernel, len(returned)),
+        norm_kernel,
         grid=(rows // tile,),
-        in_specs=[
-            pl.BlockSpec((blocks, tile, part_width), lambda step: (0, step, 0)) for _ in returned
-        ]
-        + [
-            pl.BlockSpec((tile, width), at),
-            pl.BlockSpec((1, width), lambda step: (0, 0)),
-        ],
-        out_specs=[pl.BlockSpec((tile, width), at)] * 2
-        + [pl.BlockSpec((tile, width // chunks), at)] * chunks,
-        out_shape=[pltpu.HBM((rows, width), BF)] * 2 + [shape(width // chunks)] * chunks,
+        in_specs=[pl.BlockSpec(memory_space=pltpu.SMEM)]
+        + [pl.BlockSpec((tile, piece.shape[1]), at) for piece in pieces]
+        + [whole, pl.BlockSpec((1, width), lambda step: (0, 0))],
+        out_specs=[whole] * 3,
+        out_shape=[pltpu.HBM((rows, width), BF)] * 2 + [jax.ShapeDtypeStruct((rows, width), BF)],
         compiler_params=pltpu.CompilerParams(vmem_limit_bytes=8 << 20),
-    )(*returned, patches, gain)
+    )(me, *pieces, patches, gain)
 
 
 def routing(expert_ids, gate_levels, first, experts, capacity):
@@ -347,6 +354,9 @@
     def across(value):
         return lax.ppermute(value, SEQ, mirror)
 
+    def swap(turn, value):
+        return lax.ppermute(value, SEQ, [(i, i ^ turn) for i in range(seq_count)])
+
     def exchange(axes, value):
         return lax.all_to_all(value, axes, split_axis=0, concat_axis=0, tiled=True)
 
@@ -355,8 +365,10 @@
         return exchange(HALF, sent).reshape(value.shape)
 
     other = across(jnp.concatenate([expert_ids[0], gate_levels[0]], axis=1))
-    outgoing = regroup(jnp.transpose(projected[0], (1, 0, 2)), seq_count)
-    arrived = exchange(SEQ, outgoing)
+    me = lax.axis_index(SEQ)[None]
+    arrived = list(regroup(me, jnp.transpose(projected[0], (1, 0, 2)), seq_count))
+    for turn in turns(seq_count):
+        arrived[turn] = swap(turn, arrived[turn])
     own_send, own_high, own_low = routing(
         expert_ids[0], gate_levels[0], first, half_count, capacity
     )
@@ -368,8 +380,12 @@
             (arrived, own_send, own_high, own_low, other_send, other_high, other_low)
         )
     )
-    returned = [exchange(SEQ, attention(arrived, local_heads))]
-    attended, stream, normed = residual_norm(returned, patches[0], norm_gain[None], 1)
+    returned = list(attention(me, arrived, local_heads))
+    for turn in turns(seq_count):
+        returned[turn] = swap(turn, returned[turn])
+    attended, stream, normed = residual_norm(
+        me, returned, patches[0], norm_gain[None]
+    )
 
     other_normed = across(normed)
     own_rows = routed(spread(own_send, normed))

time: 330 us -> 327 us (level)
  starting transfers between devices: 51.6 us -> 87 us
  blocking collectives: 31 us -> 0 us
  waiting for transfers between devices: 201 us -> 191 us
    ppermute x0 -> x14, waiting for transfers between devices: none -> 61.9 us  [swap(): return lax.ppermute(value, SEQ, [(i, i ^ turn) for i in range(seq_count)])]
    ppermute x3, waiting for transfers between devices: 96.2 us -> 39.3 us  [across(): return lax.ppermute(value, SEQ, mirror)]
    ppermute x0 -> x14, starting transfers between devices: none -> 32.2 us  [swap(): return lax.ppermute(value, SEQ, [(i, i ^ turn) for i in range(seq_count)])]
    all_to_all x1 -> x0, blocking collectives: 31 us -> none  [exchange(): return lax.all_to_all(value, axes, split_axis=0, concat_axis=0, tiled=True)]
    all_to_all x5 -> x4, waiting for transfers between devices: 105 us -> 89.9 us  [exchange(): return lax.all_to_all(value, axes, split_axis=0, concat_axis=0, tiled=True)]
    all_to_all x5 -> x4, starting transfers between devices: 43.3 us -> 44.1 us  [exchange(): return lax.all_to_all(value, axes, split_axis=0, concat_axis=0, tiled=True)]
  transfers between devices with their start and end apart: 8 -> 21, of which waited for: 8 -> 14; matrix products, arithmetic and copies ran while one was open for 3% -> 3% of each run, Pallas kernels for 6% -> 7%
where the time goes in v5:
time: 327 us
  waiting for transfers between devices  191 us (58%)
  starting transfers between devices  87 us (27%)
  Pallas kernels  32.7 us (10%)
  matrix products  7.75 us (2%)
  local copies, waits for them, and re-layouts  6.07 us (2%)
    all_to_all x4, waiting for transfers between devices, exchange(): return lax.all_to_all(value, axes, split_axis=0, concat_axis=0, tiled=True)  89.9 us
    ppermute x14, waiting for transfers between devices, swap(): return lax.ppermute(value, SEQ, [(i, i ^ turn) for i in range(seq_count)])  61.9 us
    all_to_all x4, starting transfers between devices, exchange(): return lax.all_to_all(value, axes, split_axis=0, concat_axis=0, tiled=True)  44.1 us
    ppermute x3, waiting for transfers between devices, across(): return lax.ppermute(value, SEQ, mirror)  39.3 us
    ppermute x14, starting transfers between devices, swap(): return lax.ppermute(value, SEQ, [(i, i ^ turn) for i in range(seq_count)])  32.2 us
    pallas_call x2, Pallas kernels, expert_ffn(): pl.pallas_call(expert_kernel, in_specs=[pl.BlockSpec(memory_space=pl.ANY)...  19 us
    ppermute x3, starting transfers between devices, across(): return lax.ppermute(value, SEQ, mirror)  10.7 us
  transfers between devices with their start and end apart: 21, of which 14 were waited for; matrix products, arithmetic and copies ran while one was open for 3% of the time, Pallas kernels for 7%

profile of v5, /device:TPU:0, one launch (start us, length us, event | category | flops | bytes accessed | tf_op | source)
XLA Modules:
  0.0 326.9 jit_solution(16113464006908086344)
XLA Ops:
  2.3 5.1 %collective-permute-start.7 = (s32[128,4]{1,0:T(8,128)S(1)}, s32[128,4]{1,0:T(8,128)S(1)}, u32[]{:S(2)}, u32[]{:S(2)}) collective-permute-start(s32[128,4]{1,0:T(8,128)S(1)} %pad_add_fusion), channel_id=1, source_target_pairs={{0,24},{4,28},{8,16},{12,20},{16,8},{20,12},{24,0},{28,4},{1,25},{... | collective-permute-start | bytes 6152 | tf_op jit(solution)/shard_map/ppermute | solution.py:355
  7.4 2.8 shard_map.95
  14.9 3.9 %collective-permute-start.4 = (bf16[3,128,512]{2,1,0:T(8,128)(2,1)}, bf16[3,128,512]{2,1,0:T(8,128)(2,1)S(1)}, u32[]{:S(2)}, u32[]{:S(2)}) collective-permute-start(bf16[3,128,512]{2,1,0:T(8,128)(2,1)} %get-tuple-element.40), channel_id=1, source_target_pairs={{0,20},{4,16},{8,28},{12,24},{16,4},{20,0},{24,12},{28,8},{1,21},{... | collective-permute-start | bytes 1179656 | tf_op jit(solution)/shard_map/ppermute | solution.py:358
  21.4 16.0 %collective-permute-done.1.refs_2_ = bf16[3,128,512]{2,1,0:T(8,128)(2,1)S(1)} collective-permute-done((bf16[3,128,512]{2,1,0:T(8,128)(2,1)}, bf16[3,128,512]{2,1,0:T(8,128)(2,1)S(1)}, u32[]{:S(2)}, u32[]{:S(2)}) %collective-permute-start.1) | collective-permute-done | bytes 393248 | tf_op jit(solution)/shard_map/ppermute | solution.py:358
  39.6 3.6 %collective-permute-done.2.refs_3_ = bf16[3,128,512]{2,1,0:T(8,128)(2,1)S(1)} collective-permute-done((bf16[3,128,512]{2,1,0:T(8,128)(2,1)}, bf16[3,128,512]{2,1,0:T(8,128)(2,1)S(1)}, u32[]{:S(2)}, u32[]{:S(2)}) %collective-permute-start.2) | collective-permute-done | bytes 393248 | tf_op jit(solution)/shard_map/ppermute | solution.py:358
  43.2 26.8 %collective-permute-done.4.refs_5_ = bf16[3,128,512]{2,1,0:T(8,128)(2,1)S(1)} collective-permute-done((bf16[3,128,512]{2,1,0:T(8,128)(2,1)}, bf16[3,128,512]{2,1,0:T(8,128)(2,1)S(1)}, u32[]{:S(2)}, u32[]{:S(2)}) %collective-permute-start.4) | collective-permute-done | bytes 393248 | tf_op jit(solution)/shard_map/ppermute | solution.py:358
  71.0 6.1 %shard_map.96 = (bf16[128,512]{1,0:T(8,128)(2,1)}, bf16[128,512]{1,0:T(8,128)(2,1)}, bf16[128,512]{1,0:T(8,128)(2,1)}, bf16[128,512]{1,0:T(8,128)(2,1)}, bf16[12...) custom-call(s32[1]{0:T(128)} %bitcast.me_ref, ...), custom_call_target="tpu_custom_call" | custom-call | flops 1073741824 | bytes 4194304 | tf_op jit(solution)/shard_map/pallas_call | solution.py:93
  77.6 15.2 %collective-permute-start.9 = (bf16[128,512]{1,0:T(8,128)(2,1)}, bf16[128,512]{1,0:T(8,128)(2,1)S(1)}, u32[]{:S(2)}, u32[]{:S(2)}) collective-permute-start(bf16[128,512]{1,0:T(8,128)(2,1)} %get-tuple-element.53), channel_id=1, source_target_pairs={{0,8},{4,12},{8,0},{12,4},{16,24},{20,28},{24,16},{28,20},{1,9},{5... | collective-permute-start | bytes 393224 | tf_op jit(solution)/shard_map/ppermute | solution.py:358
  101.7 9.6 %collective-permute-done.11.refs_4_ = bf16[128,512]{1,0:T(8,128)(2,1)S(1)} collective-permute-done((bf16[128,512]{1,0:T(8,128)(2,1)}, bf16[128,512]{1,0:T(8,128)(2,1)S(1)}, u32[]{:S(2)}, u32[]{:S(2)}) %collective-permute-start.11) | collective-permute-done | bytes 131104 | tf_op jit(solution)/shard_map/ppermute | solution.py:358
  111.3 2.8 collective-permute-done.12.refs_5_
  118.9 18.1 %collective-permute-done.15 = bf16[128,4096]{1,0:T(8,128)(2,1)S(1)} collective-permute-done((bf16[128,4096]{1,0:T(8,128)(2,1)S(1)}, bf16[128,4096]{1,0:T(8,128)(2,1)S(1)}, u32[]{:S(2)}, u32[]{:S(2)}) %collective-permute-start.15) | collective-permute-done | bytes 1048608 | tf_op jit(solution)/shard_map/ppermute | solution.py:355
  139.0 32.1 %all-to-all-start.2 = ((bf16[16,16,4096]{2,1,0:T(8,128)(2,1)}), bf16[16,16,4096]{2,1,0:T(8,128)(2,1)S(1)}, u32[]{:S(2)}, u32[]{:S(2)}) async-start(bf16[16,16,4096]{2,1,0:T(8,128)(2,1)} %bitcast.37), calls=%async_computation.2 | async-start | bytes 4194304 | tf_op jit(solution)/shard_map/all_to_all | solution.py:361
  173.2 27.6 %all-to-all-done.2 = bf16[16,16,4096]{2,1,0:T(8,128)(2,1)S(1)} async-done(((bf16[16,16,4096]{2,1,0:T(8,128)(2,1)}), bf16[16,16,4096]{2,1,0:T(8,128)(2,1)S(1)}, u32[]{:S(2)}, u32[]{:S(2)}) %all-to-all-start.2) | async-done | bytes 2097184 | tf_op jit(solution)/shard_map/all_to_all | solution.py:361
  200.7 4.4 %all-to-all-start = ((bf16[16,16,4096]{2,1,0:T(8,128)(2,1)}), bf16[16,16,4096]{2,1,0:T(8,128)(2,1)}, u32[]{:S(2)}, u32[]{:S(2)}) async-start(bf16[16,16,4096]{2,1,0:T(8,128)(2,1)} %bitcast.36), calls=%async_computation | async-start | bytes 4194304 | tf_op jit(solution)/shard_map/all_to_all | solution.py:361
  205.2 9.2 %shard_map.99 = bf16[256,4096]{1,0:T(8,128)(2,1)} custom-call(bf16[256,4096]{1,0:T(8,128)(2,1)S(1)} %bitcast.31, bf16[1,4096,768]{2,1,0:T(8,128)(2,1)} %gate_hbm.3, bf16[1,4096,768]{2,1,0:T(8,128)(2,1)} %up_hbm.3, bf16[1,768,4096]{2,1,0:T(8,128)(2,1)} %down_hbm.3), custom_call_target="tpu_custom_call" | custom-call | flops 4831838208 | bytes 23068672 | tf_op jit(solution)/shard_map/pallas_call | solution.py:177
  214.4 20.4 %all-to-all-done = bf16[16,16,4096]{2,1,0:T(8,128)(2,1)} async-done(((bf16[16,16,4096]{2,1,0:T(8,128)(2,1)}), bf16[16,16,4096]{2,1,0:T(8,128)(2,1)}, u32[]{:S(2)}, u32[]{:S(2)}) %all-to-all-start) | async-done | bytes 2097184 | tf_op jit(solution)/shard_map/all_to_all | solution.py:361
  234.9 3.9 %all-to-all-start.3 = ((bf16[16,16,4096]{2,1,0:T(8,128)(2,1)}), bf16[16,16,4096]{2,1,0:T(8,128)(2,1)S(1)}, u32[]{:S(2)}, u32[]{:S(2)}) async-start(bf16[16,16,4096]{2,1,0:T(8,128)(2,1)} %bitcast.39), calls=%async_computation.3 | async-start | bytes 4194304 | tf_op jit(solution)/shard_map/all_to_all | solution.py:361
  238.8 9.8 %shard_map.98 = bf16[256,4096]{1,0:T(8,128)(2,1)} custom-call(bf16[256,4096]{1,0:T(8,128)(2,1)} %bitcast.9.rows_hbm, bf16[1,4096,768]{2,1,0:T(8,128)(2,1)} %gate_hbm.3, bf16[1,4096,768]{2,1,0:T(8,128)(2,1)} %up_hbm.3, bf16[1,768,4096]{2,1,0:T(8,128)(2,1)} %down_hbm.3), custom_call_target="tpu_custom_call" | custom-call | flops 4831838208 | bytes 23068672 | tf_op jit(solution)/shard_map/pallas_call | solution.py:177
  248.6 19.7 %all-to-all-done.3 = bf16[16,16,4096]{2,1,0:T(8,128)(2,1)S(1)} async-done(((bf16[16,16,4096]{2,1,0:T(8,128)(2,1)}), bf16[16,16,4096]{2,1,0:T(8,128)(2,1)S(1)}, u32[]{:S(2)}, u32[]{:S(2)}) %all-to-all-start.3) | async-done | bytes 2097184 | tf_op jit(solution)/shard_map/all_to_all | solution.py:361
  269.5 3.7 %all-to-all-start.1 = ((bf16[16,16,4096]{2,1,0:T(8,128)(2,1)}), bf16[16,16,4096]{2,1,0:T(8,128)(2,1)S(1)}, u32[]{:S(2)}, u32[]{:S(2)}) async-start(bf16[16,16,4096]{2,1,0:T(8,128)(2,1)} %bitcast.38), calls=%async_computation.1 | async-start | bytes 4194304 | tf_op jit(solution)/shard_map/all_to_all | solution.py:361
  276.9 3.7 %collective-permute-start.16 = (bf16[128,4096]{1,0:T(8,128)(2,1)}, bf16[128,4096]{1,0:T(8,128)(2,1)}, u32[]{:S(2)}, u32[]{:S(2)}) collective-permute-start(bf16[128,4096]{1,0:T(8,128)(2,1)} %fusion), channel_id=1, source_target_pairs={{0,24},{4,28},{8,16},{12,20},{16,8},{20,12},{24,0},{28,4},{1,25},{... | collective-permute-start | bytes 3145736 | tf_op jit(solution)/shard_map/ppermute | solution.py:355
  280.6 22.2 %all-to-all-done.1 = bf16[16,16,4096]{2,1,0:T(8,128)(2,1)S(1)} async-done(((bf16[16,16,4096]{2,1,0:T(8,128)(2,1)}), bf16[16,16,4096]{2,1,0:T(8,128)(2,1)S(1)}, u32[]{:S(2)}, u32[]{:S(2)}) %all-to-all-start.1) | async-done | bytes 2097184 | tf_op jit(solution)/shard_map/all_to_all | solution.py:361
  302.9 21.1 %collective-permute-done.16.other_ref = bf16[128,4096]{1,0:T(8,128)(2,1)} collective-permute-done((bf16[128,4096]{1,0:T(8,128)(2,1)}, bf16[128,4096]{1,0:T(8,128)(2,1)}, u32[]{:S(2)}, u32[]{:S(2)}) %collective-permute-start.16) | collective-permute-done | bytes 1048608 | tf_op jit(solution)/shard_map/ppermute | solution.py:355
  324.0 2.7 shard_map.100
  (63 shorter events, 35.2 us)
Async XLA Ops:
  2.3 12.6 %collective-permute-start.7 = (s32[128,4]{1,0:T(8,128)S(1)}, s32[128,4]{1,0:T(8,128)S(1)}, u32[]{:S(2)}, u32[]{:S(2)}) collective-permute-start(s32[128,4]{1,0:T(8,128)S(1)} %pad_add_fusion), channel_id=1, source_target_pairs={{0,24},{4,28},{8,16},{12,20},{16,8},{20,12},{24,0},{28,4},{1,25},{... | collective-permute-start | bytes 6152 | tf_op jit(solution)/shard_map/ppermute | solution.py:355
  10.3 10.9 %collective-permute-start = (bf16[3,128,512]{2,1,0:T(8,128)(2,1)}, bf16[3,128,512]{2,1,0:T(8,128)(2,1)S(1)}, u32[]{:S(2)}, u32[]{:S(2)}) collective-permute-start(bf16[3,128,512]{2,1,0:T(8,128)(2,1)} %get-tuple-element.36), channel_id=1, source_target_pairs={{0,4},{4,0},{8,12},{12,8},{16,20},{20,16},{24,28},{28,24},{1,5},{5... | collective-permute-start | bytes 1179656 | tf_op jit(solution)/shard_map/ppermute | solution.py:358
  11.8 25.6 %collective-permute-start.1 = (bf16[3,128,512]{2,1,0:T(8,128)(2,1)}, bf16[3,128,512]{2,1,0:T(8,128)(2,1)S(1)}, u32[]{:S(2)}, u32[]{:S(2)}) collective-permute-start(bf16[3,128,512]{2,1,0:T(8,128)(2,1)} %get-tuple-element.37), channel_id=1, source_target_pairs={{0,8},{4,12},{8,0},{12,4},{16,24},{20,28},{24,16},{28,20},{1,9},{5... | collective-permute-start | bytes 1179656 | tf_op jit(solution)/shard_map/ppermute | solution.py:358
  11.8 31.4 %collective-permute-start.2 = (bf16[3,128,512]{2,1,0:T(8,128)(2,1)}, bf16[3,128,512]{2,1,0:T(8,128)(2,1)S(1)}, u32[]{:S(2)}, u32[]{:S(2)}) collective-permute-start(bf16[3,128,512]{2,1,0:T(8,128)(2,1)} %get-tuple-element.38), channel_id=1, source_target_pairs={{0,12},{4,8},{8,4},{12,0},{16,28},{20,24},{24,20},{28,16},{1,13},{... | collective-permute-start | bytes 1179656 | tf_op jit(solution)/shard_map/ppermute | solution.py:358
  13.8 29.4 %collective-permute-start.3 = (bf16[3,128,512]{2,1,0:T(8,128)(2,1)}, bf16[3,128,512]{2,1,0:T(8,128)(2,1)S(1)}, u32[]{:S(2)}, u32[]{:S(2)}) collective-permute-start(bf16[3,128,512]{2,1,0:T(8,128)(2,1)} %get-tuple-element.39), channel_id=1, source_target_pairs={{0,16},{4,20},{8,24},{12,28},{16,0},{20,4},{24,8},{28,12},{1,17},{... | collective-permute-start | bytes 1179656 | tf_op jit(solution)/shard_map/ppermute | solution.py:358
  14.9 55.1 %collective-permute-start.4 = (bf16[3,128,512]{2,1,0:T(8,128)(2,1)}, bf16[3,128,512]{2,1,0:T(8,128)(2,1)S(1)}, u32[]{:S(2)}, u32[]{:S(2)}) collective-permute-start(bf16[3,128,512]{2,1,0:T(8,128)(2,1)} %get-tuple-element.40), channel_id=1, source_target_pairs={{0,20},{4,16},{8,28},{12,24},{16,4},{20,0},{24,12},{28,8},{1,21},{... | collective-permute-start | bytes 1179656 | tf_op jit(solution)/shard_map/ppermute | solution.py:358
  21.1 48.9 %collective-permute-start.5 = (bf16[3,128,512]{2,1,0:T(8,128)(2,1)}, bf16[3,128,512]{2,1,0:T(8,128)(2,1)S(1)}, u32[]{:S(2)}, u32[]{:S(2)}) collective-permute-start(bf16[3,128,512]{2,1,0:T(8,128)(2,1)} %get-tuple-element.41), channel_id=1, source_target_pairs={{0,24},{4,28},{8,16},{12,20},{16,8},{20,12},{24,0},{28,4},{1,25},{... | collective-permute-start | bytes 1179656 | tf_op jit(solution)/shard_map/ppermute | solution.py:358
  37.5 32.5 %collective-permute-start.6 = (bf16[3,128,512]{2,1,0:T(8,128)(2,1)}, bf16[3,128,512]{2,1,0:T(8,128)(2,1)S(1)}, u32[]{:S(2)}, u32[]{:S(2)}) collective-permute-start(bf16[3,128,512]{2,1,0:T(8,128)(2,1)} %get-tuple-element.42), channel_id=1, source_target_pairs={{0,28},{4,24},{8,20},{12,16},{16,12},{20,8},{24,4},{28,0},{1,29},{... | collective-permute-start | bytes 1179656 | tf_op jit(solution)/shard_map/ppermute | solution.py:358
  39.4 74.7 %copy-start = (bf16[1,128,4096]{2,1,0:T(8,128)(2,1)S(1)}, bf16[1,128,4096]{2,1,0:T(8,128)(2,1)}, u32[]{:S(2)}) copy-start(bf16[1,128,4096]{2,1,0:T(8,128)(2,1)} %param.9) | copy-start | bytes 3145732
  39.4 74.7 %copy-start.3 = (f32[4096]{0:T(1024)S(1)}, f32[4096]{0:T(1024)}, u32[]{:S(2)}) copy-start(f32[4096]{0:T(1024)} %param.10) | copy-start | bytes 49156
  77.0 19.6 %collective-permute-start.8 = (bf16[128,512]{1,0:T(8,128)(2,1)}, bf16[128,512]{1,0:T(8,128)(2,1)S(1)}, u32[]{:S(2)}, u32[]{:S(2)}) collective-permute-start(bf16[128,512]{1,0:T(8,128)(2,1)} %get-tuple-element.52), channel_id=1, source_target_pairs={{0,4},{4,0},{8,12},{12,8},{16,20},{20,16},{24,28},{28,24},{1,5},{5... | collective-permute-start | bytes 393224 | tf_op jit(solution)/shard_map/ppermute | solution.py:358
  77.6 22.1 %collective-permute-start.9 = (bf16[128,512]{1,0:T(8,128)(2,1)}, bf16[128,512]{1,0:T(8,128)(2,1)S(1)}, u32[]{:S(2)}, u32[]{:S(2)}) collective-permute-start(bf16[128,512]{1,0:T(8,128)(2,1)} %get-tuple-element.53), channel_id=1, source_target_pairs={{0,8},{4,12},{8,0},{12,4},{16,24},{20,28},{24,16},{28,20},{1,9},{5... | collective-permute-start | bytes 393224 | tf_op jit(solution)/shard_map/ppermute | solution.py:358
  92.8 8.8 %collective-permute-start.10 = (bf16[128,512]{1,0:T(8,128)(2,1)}, bf16[128,512]{1,0:T(8,128)(2,1)S(1)}, u32[]{:S(2)}, u32[]{:S(2)}) collective-permute-start(bf16[128,512]{1,0:T(8,128)(2,1)} %get-tuple-element.54), channel_id=1, source_target_pairs={{0,12},{4,8},{8,4},{12,0},{16,28},{20,24},{24,20},{28,16},{1,13},{... | collective-permute-start | bytes 393224 | tf_op jit(solution)/shard_map/ppermute | solution.py:358
  93.8 17.5 %collective-permute-start.11 = (bf16[128,512]{1,0:T(8,128)(2,1)}, bf16[128,512]{1,0:T(8,128)(2,1)S(1)}, u32[]{:S(2)}, u32[]{:S(2)}) collective-permute-start(bf16[128,512]{1,0:T(8,128)(2,1)} %get-tuple-element.55), channel_id=1, source_target_pairs={{0,16},{4,20},{8,24},{12,28},{16,0},{20,4},{24,8},{28,12},{1,17},{... | collective-permute-start | bytes 393224 | tf_op jit(solution)/shard_map/ppermute | solution.py:358
  94.7 19.4 %collective-permute-start.12 = (bf16[128,512]{1,0:T(8,128)(2,1)}, bf16[128,512]{1,0:T(8,128)(2,1)S(1)}, u32[]{:S(2)}, u32[]{:S(2)}) collective-permute-start(bf16[128,512]{1,0:T(8,128)(2,1)} %get-tuple-element.56), channel_id=1, source_target_pairs={{0,20},{4,16},{8,28},{12,24},{16,4},{20,0},{24,12},{28,8},{1,21},{... | collective-permute-start | bytes 393224 | tf_op jit(solution)/shard_map/ppermute | solution.py:358
  96.7 17.4 %collective-permute-start.13 = (bf16[128,512]{1,0:T(8,128)(2,1)}, bf16[128,512]{1,0:T(8,128)(2,1)S(1)}, u32[]{:S(2)}, u32[]{:S(2)}) collective-permute-start(bf16[128,512]{1,0:T(8,128)(2,1)} %get-tuple-element.57), channel_id=1, source_target_pairs={{0,24},{4,28},{8,16},{12,20},{16,8},{20,12},{24,0},{28,4},{1,25},{... | collective-permute-start | bytes 393224 | tf_op jit(solution)/shard_map/ppermute | solution.py:358
  99.7 14.3 %collective-permute-start.14 = (bf16[128,512]{1,0:T(8,128)(2,1)}, bf16[128,512]{1,0:T(8,128)(2,1)S(1)}, u32[]{:S(2)}, u32[]{:S(2)}) collective-permute-start(bf16[128,512]{1,0:T(8,128)(2,1)} %get-tuple-element.58), channel_id=1, source_target_pairs={{0,28},{4,24},{8,20},{12,16},{16,12},{20,8},{24,4},{28,0},{1,29},{... | collective-permute-start | bytes 393224 | tf_op jit(solution)/shard_map/ppermute | solution.py:358
  117.0 20.0 %collective-permute-start.15 = (bf16[128,4096]{1,0:T(8,128)(2,1)S(1)}, bf16[128,4096]{1,0:T(8,128)(2,1)S(1)}, u32[]{:S(2)}, u32[]{:S(2)}) collective-permute-start(bf16[128,4096]{1,0:T(8,128)(2,1)S(1)} %get-tuple-element.63), channel_id=1, source_target_pairs={{0,24},{4,28},{8,16},{12,20},{16,8},{20,12},{24,0},{28,4},{1,25},{... | collective-permute-start | bytes 3145736 | tf_op jit(solution)/shard_map/ppermute | solution.py:355
  139.0 61.7 %all-to-all-start.2 = ((bf16[16,16,4096]{2,1,0:T(8,128)(2,1)}), bf16[16,16,4096]{2,1,0:T(8,128)(2,1)S(1)}, u32[]{:S(2)}, u32[]{:S(2)}) async-start(bf16[16,16,4096]{2,1,0:T(8,128)(2,1)} %bitcast.37), calls=%async_computation.2 | async-start | bytes 4194304 | tf_op jit(solution)/shard_map/all_to_all | solution.py:361
  200.7 34.1 %all-to-all-start = ((bf16[16,16,4096]{2,1,0:T(8,128)(2,1)}), bf16[16,16,4096]{2,1,0:T(8,128)(2,1)}, u32[]{:S(2)}, u32[]{:S(2)}) async-start(bf16[16,16,4096]{2,1,0:T(8,128)(2,1)} %bitcast.36), calls=%async_computation | async-start | bytes 4194304 | tf_op jit(solution)/shard_map/all_to_all | solution.py:361
  234.9 33.4 %all-to-all-start.3 = ((bf16[16,16,4096]{2,1,0:T(8,128)(2,1)}), bf16[16,16,4096]{2,1,0:T(8,128)(2,1)S(1)}, u32[]{:S(2)}, u32[]{:S(2)}) async-start(bf16[16,16,4096]{2,1,0:T(8,128)(2,1)} %bitcast.39), calls=%async_computation.3 | async-start | bytes 4194304 | tf_op jit(solution)/shard_map/all_to_all | solution.py:361
  269.5 33.4 %all-to-all-start.1 = ((bf16[16,16,4096]{2,1,0:T(8,128)(2,1)}), bf16[16,16,4096]{2,1,0:T(8,128)(2,1)S(1)}, u32[]{:S(2)}, u32[]{:S(2)}) async-start(bf16[16,16,4096]{2,1,0:T(8,128)(2,1)} %bitcast.38), calls=%async_computation.1 | async-start | bytes 4194304 | tf_op jit(solution)/shard_map/all_to_all | solution.py:361
  275.5 48.6 %copy-start.1 = (bf16[128,4096]{1,0:T(8,128)(2,1)S(1)}, bf16[128,4096]{1,0:T(8,128)(2,1)}, u32[]{:S(2)}) copy-start(bf16[128,4096]{1,0:T(8,128)(2,1)} %get-tuple-element.64.stream_ref) | copy-start | bytes 3145732
  276.9 47.1 %collective-permute-start.16 = (bf16[128,4096]{1,0:T(8,128)(2,1)}, bf16[128,4096]{1,0:T(8,128)(2,1)}, u32[]{:S(2)}, u32[]{:S(2)}) collective-permute-start(bf16[128,4096]{1,0:T(8,128)(2,1)} %fusion), channel_id=1, source_target_pairs={{0,24},{4,28},{8,16},{12,20},{16,8},{20,12},{24,0},{28,4},{1,25},{... | collective-permute-start | bytes 3145736 | tf_op jit(solution)/shard_map/ppermute | solution.py:355
  (4 other events, 5.4 us)

commit v6 on v5

--- a/solution.py
+++ b/solution.py
@@ -199,17 +199,17 @@
     )(rows, in_hbm(w_gate), in_hbm(w_up), in_hbm(w_down))
 
 
-def regroup_kernel(me_ref, in_ref, *refs):
+def regroup_kernel(chosen, me_ref, in_ref, *refs):
     *out_refs, held, arrived, left = refs
     _, _, _, local_width = held.shape
     reads, writes = [], []
-    for turn, out_ref in enumerate(out_refs):
+    for index, (turn, out_ref) in enumerate(zip(chosen, out_refs)):
         block = jnp.bitwise_xor(me_ref[0], turn)
         columns = pl.ds(pl.multiple_of(block * local_width, local_width), local_width)
         reads.append(
-            pltpu.make_async_copy(in_ref.at[:, :, columns], held.at[turn], arrived.at[turn])
+            pltpu.make_async_copy(in_ref.at[:, :, columns], held.at[index], arrived.at[index])
         )
-        writes.append(pltpu.make_async_copy(held.at[turn], out_ref, left.at[turn]))
+        writes.append(pltpu.make_async_copy(held.at[index], out_ref, left.at[index]))
     for read in reads:
         read.start()
     for read, write in zip(reads, writes):
@@ -219,12 +219,13 @@
         write.wait()
 
 
-def regroup(me, projected, blocks):
+def regroup(me, projected, blocks, chosen):
     kinds, rows, width = projected.shape
     shape = (kinds, rows, width // blocks)
+    blocks = len(chosen)
     hbm = pl.BlockSpec(memory_space=pltpu.HBM)
     return pl.pallas_call(
-        regroup_kernel,
+        functools.partial(regroup_kernel, chosen),
         in_specs=[pl.BlockSpec(memory_space=pltpu.SMEM), hbm],
         out_specs=[hbm] * blocks,
         out_shape=[pltpu.HBM(shape, BF)] * blocks,
@@ -366,9 +367,13 @@
 
     other = across(jnp.concatenate([expert_ids[0], gate_levels[0]], axis=1))
     me = lax.axis_index(SEQ)[None]
-    arrived = list(regroup(me, jnp.transpose(projected[0], (1, 0, 2)), seq_count))
-    for turn in turns(seq_count):
-        arrived[turn] = swap(turn, arrived[turn])
+    kinds = jnp.transpose(projected[0], (1, 0, 2))
+    first_turn, *later = turns(seq_count)
+    later = tuple(later) + (0,)
+    (head,) = regroup(me, kinds, seq_count, (first_turn,))
+    rest = regroup(me, kinds, seq_count, later)
+    arrived = {turn: piece for turn, piece in zip((first_turn,) + later, (head, *rest))}
+    arrived = [swap(turn, arrived[turn]) if turn else arrived[turn] for turn in range(seq_count)]
     own_send, own_high, own_low = routing(
         expert_ids[0], gate_levels[0], first, half_count, capacity
     )

time: 327 us -> 323 us (0.988)
  starting transfers between devices: 87 us -> 82.1 us
    all_to_all x4, waiting for transfers between devices: 89.9 us -> 115 us  [exchange(): return lax.all_to_all(value, axes, split_axis=0, concat_axis=0, tiled=True)]
    ppermute x3, waiting for transfers between devices: 39.3 us -> 21.1 us  [across(): return lax.ppermute(value, SEQ, mirror)]
    ppermute x14, waiting for transfers between devices: 61.9 us -> 54.6 us  [swap(): return lax.ppermute(value, SEQ, [(i, i ^ turn) for i in range(seq_count)])]
    all_to_all x4, starting transfers between devices: 44.1 us -> 39.8 us  [exchange(): return lax.all_to_all(value, axes, split_axis=0, concat_axis=0, tiled=True)]
  transfers between devices with their start and end apart: 21 -> 21, of which waited for: 14 -> 11; matrix products, arithmetic and copies ran while one was open for 3% -> 3% of each run, Pallas kernels for 7% -> 7%
where the time goes in v6:
time: 323 us
  waiting for transfers between devices  190 us (59%)
  starting transfers between devices  82.1 us (25%)
  Pallas kernels  34.3 us (11%)
  matrix products  7.74 us (2%)
  local copies, waits for them, and re-layouts  6.07 us (2%)
    all_to_all x4, waiting for transfers between devices, exchange(): return lax.all_to_all(value, axes, split_axis=0, concat_axis=0, tiled=True)  115 us
    ppermute x14, waiting for transfers between devices, swap(): return lax.ppermute(value, SEQ, [(i, i ^ turn) for i in range(seq_count)])  54.6 us
    all_to_all x4, starting transfers between devices, exchange(): return lax.all_to_all(value, axes, split_axis=0, concat_axis=0, tiled=True)  39.8 us
    ppermute x14, starting transfers between devices, swap(): return lax.ppermute(value, SEQ, [(i, i ^ turn) for i in range(seq_count)])  33.7 us
    ppermute x3, waiting for transfers between devices, across(): return lax.ppermute(value, SEQ, mirror)  21.1 us
    pallas_call x2, Pallas kernels, expert_ffn(): pl.pallas_call(expert_kernel, in_specs=[pl.BlockSpec(memory_space=pl.ANY)...  19 us
    ppermute x3, starting transfers between devices, across(): return lax.ppermute(value, SEQ, mirror)  8.63 us
  transfers between devices with their start and end apart: 21, of which 11 were waited for; matrix products, arithmetic and copies ran while one was open for 3% of the time, Pallas kernels for 7%

profile of v6, /device:TPU:0, one launch (start us, length us, event | category | flops | bytes accessed | tf_op | source)
XLA Modules:
  0.0 322.8 jit_solution(18446016727898517066)
XLA Ops:
  2.3 5.1 %collective-permute-start.7 = (s32[128,4]{1,0:T(8,128)S(1)}, s32[128,4]{1,0:T(8,128)S(1)}, u32[]{:S(2)}, u32[]{:S(2)}) collective-permute-start(s32[128,4]{1,0:T(8,128)S(1)} %pad_add_fusion), channel_id=1, source_target_pairs={{0,24},{4,28},{8,16},{12,20},{16,8},{20,12},{24,0},{28,4},{1,25},{... | collective-permute-start | bytes 6152 | tf_op jit(solution)/shard_map/ppermute | solution.py:356
  9.3 2.6 shard_map.95
  20.1 3.3 %collective-permute-done.5.refs_6_ = bf16[3,128,512]{2,1,0:T(8,128)(2,1)S(1)} collective-permute-done((bf16[3,128,512]{2,1,0:T(8,128)(2,1)}, bf16[3,128,512]{2,1,0:T(8,128)(2,1)S(1)}, u32[]{:S(2)}, u32[]{:S(2)}) %collective-permute-start.5) | collective-permute-done | bytes 393248 | tf_op jit(solution)/shard_map/ppermute | solution.py:359
  23.3 7.0 %collective-permute-start.4 = (bf16[3,128,512]{2,1,0:T(8,128)(2,1)}, bf16[3,128,512]{2,1,0:T(8,128)(2,1)S(1)}, u32[]{:S(2)}, u32[]{:S(2)}) collective-permute-start(bf16[3,128,512]{2,1,0:T(8,128)(2,1)} %get-tuple-element.39), channel_id=1, source_target_pairs={{0,20},{4,16},{8,28},{12,24},{16,4},{20,0},{24,12},{28,8},{1,21},{... | collective-permute-start | bytes 1179656 | tf_op jit(solution)/shard_map/ppermute | solution.py:359
  33.3 8.6 %collective-permute-done.1.refs_2_ = bf16[3,128,512]{2,1,0:T(8,128)(2,1)S(1)} collective-permute-done((bf16[3,128,512]{2,1,0:T(8,128)(2,1)}, bf16[3,128,512]{2,1,0:T(8,128)(2,1)S(1)}, u32[]{:S(2)}, u32[]{:S(2)}) %collective-permute-start.1) | collective-permute-done | bytes 393248 | tf_op jit(solution)/shard_map/ppermute | solution.py:359
  41.9 9.3 %collective-permute-done.2.refs_3_ = bf16[3,128,512]{2,1,0:T(8,128)(2,1)S(1)} collective-permute-done((bf16[3,128,512]{2,1,0:T(8,128)(2,1)}, bf16[3,128,512]{2,1,0:T(8,128)(2,1)S(1)}, u32[]{:S(2)}, u32[]{:S(2)}) %collective-permute-start.2) | collective-permute-done | bytes 393248 | tf_op jit(solution)/shard_map/ppermute | solution.py:359
  51.1 20.9 %collective-permute-done.4.refs_5_ = bf16[3,128,512]{2,1,0:T(8,128)(2,1)S(1)} collective-permute-done((bf16[3,128,512]{2,1,0:T(8,128)(2,1)}, bf16[3,128,512]{2,1,0:T(8,128)(2,1)S(1)}, u32[]{:S(2)}, u32[]{:S(2)}) %collective-permute-start.4) | collective-permute-done | bytes 393248 | tf_op jit(solution)/shard_map/ppermute | solution.py:359
  73.0 6.1 %shard_map.97 = (bf16[128,512]{1,0:T(8,128)(2,1)}, bf16[128,512]{1,0:T(8,128)(2,1)}, bf16[128,512]{1,0:T(8,128)(2,1)}, bf16[128,512]{1,0:T(8,128)(2,1)}, bf16[12...) custom-call(s32[1]{0:T(128)} %bitcast.me_ref, ...), custom_call_target="tpu_custom_call" | custom-call | flops 1073741824 | bytes 4194304 | tf_op jit(solution)/shard_map/pallas_call | solution.py:93
  79.7 7.6 %collective-permute-start.9 = (bf16[128,512]{1,0:T(8,128)(2,1)}, bf16[128,512]{1,0:T(8,128)(2,1)S(1)}, u32[]{:S(2)}, u32[]{:S(2)}) collective-permute-start(bf16[128,512]{1,0:T(8,128)(2,1)} %get-tuple-element.51), channel_id=1, source_target_pairs={{0,8},{4,12},{8,0},{12,4},{16,24},{20,28},{24,16},{28,20},{1,9},{5... | collective-permute-start | bytes 393224 | tf_op jit(solution)/shard_map/ppermute | solution.py:359
  88.2 3.0 collective-permute-start.11
  94.2 3.8 %collective-permute-start.14 = (bf16[128,512]{1,0:T(8,128)(2,1)}, bf16[128,512]{1,0:T(8,128)(2,1)S(1)}, u32[]{:S(2)}, u32[]{:S(2)}) collective-permute-start(bf16[128,512]{1,0:T(8,128)(2,1)} %get-tuple-element.56), channel_id=1, source_target_pairs={{0,28},{4,24},{8,20},{12,16},{16,12},{20,8},{24,4},{28,0},{1,29},{... | collective-permute-start | bytes 393224 | tf_op jit(solution)/shard_map/ppermute | solution.py:359
  98.0 11.9 %collective-permute-done.12.refs_5_ = bf16[128,512]{1,0:T(8,128)(2,1)S(1)} collective-permute-done((bf16[128,512]{1,0:T(8,128)(2,1)}, bf16[128,512]{1,0:T(8,128)(2,1)S(1)}, u32[]{:S(2)}, u32[]{:S(2)}) %collective-permute-start.12) | collective-permute-done | bytes 131104 | tf_op jit(solution)/shard_map/ppermute | solution.py:359
  114.7 21.1 %collective-permute-done.15 = bf16[128,4096]{1,0:T(8,128)(2,1)S(1)} collective-permute-done((bf16[128,4096]{1,0:T(8,128)(2,1)S(1)}, bf16[128,4096]{1,0:T(8,128)(2,1)S(1)}, u32[]{:S(2)}, u32[]{:S(2)}) %collective-permute-start.15) | collective-permute-done | bytes 1048608 | tf_op jit(solution)/shard_map/ppermute | solution.py:356
  137.9 27.8 %all-to-all-start.2 = ((bf16[16,16,4096]{2,1,0:T(8,128)(2,1)}), bf16[16,16,4096]{2,1,0:T(8,128)(2,1)S(1)}, u32[]{:S(2)}, u32[]{:S(2)}) async-start(bf16[16,16,4096]{2,1,0:T(8,128)(2,1)} %bitcast.39), calls=%async_computation.2 | async-start | bytes 4194304 | tf_op jit(solution)/shard_map/all_to_all | solution.py:362
  167.7 27.6 %all-to-all-done.2 = bf16[16,16,4096]{2,1,0:T(8,128)(2,1)S(1)} async-done(((bf16[16,16,4096]{2,1,0:T(8,128)(2,1)}), bf16[16,16,4096]{2,1,0:T(8,128)(2,1)S(1)}, u32[]{:S(2)}, u32[]{:S(2)}) %all-to-all-start.2) | async-done | bytes 2097184 | tf_op jit(solution)/shard_map/all_to_all | solution.py:362
  195.3 4.4 %all-to-all-start = ((bf16[16,16,4096]{2,1,0:T(8,128)(2,1)}), bf16[16,16,4096]{2,1,0:T(8,128)(2,1)}, u32[]{:S(2)}, u32[]{:S(2)}) async-start(bf16[16,16,4096]{2,1,0:T(8,128)(2,1)} %bitcast.38), calls=%async_computation | async-start | bytes 4194304 | tf_op jit(solution)/shard_map/all_to_all | solution.py:362
  199.8 9.2 %shard_map.100 = bf16[256,4096]{1,0:T(8,128)(2,1)} custom-call(bf16[256,4096]{1,0:T(8,128)(2,1)S(1)} %bitcast.31, bf16[1,4096,768]{2,1,0:T(8,128)(2,1)} %gate_hbm.3, bf16[1,4096,768]{2,1,0:T(8,128)(2,1)} %up_hbm.3, bf16[1,768,4096]{2,1,0:T(8,128)(2,1)} %down_hbm.3), custom_call_target="tpu_custom_call" | custom-call | flops 4831838208 | bytes 23068672 | tf_op jit(solution)/shard_map/pallas_call | solution.py:177
  209.0 20.4 %all-to-all-done = bf16[16,16,4096]{2,1,0:T(8,128)(2,1)} async-done(((bf16[16,16,4096]{2,1,0:T(8,128)(2,1)}), bf16[16,16,4096]{2,1,0:T(8,128)(2,1)}, u32[]{:S(2)}, u32[]{:S(2)}) %all-to-all-start) | async-done | bytes 2097184 | tf_op jit(solution)/shard_map/all_to_all | solution.py:362
  229.4 3.9 %all-to-all-start.3 = ((bf16[16,16,4096]{2,1,0:T(8,128)(2,1)}), bf16[16,16,4096]{2,1,0:T(8,128)(2,1)S(1)}, u32[]{:S(2)}, u32[]{:S(2)}) async-start(bf16[16,16,4096]{2,1,0:T(8,128)(2,1)} %bitcast.41), calls=%async_computation.3 | async-start | bytes 4194304 | tf_op jit(solution)/shard_map/all_to_all | solution.py:362
  233.3 9.8 %shard_map.99 = bf16[256,4096]{1,0:T(8,128)(2,1)} custom-call(bf16[256,4096]{1,0:T(8,128)(2,1)} %bitcast.10.rows_hbm, bf16[1,4096,768]{2,1,0:T(8,128)(2,1)} %gate_hbm.3, bf16[1,4096,768]{2,1,0:T(8,128)(2,1)} %up_hbm.3, bf16[1,768,4096]{2,1,0:T(8,128)(2,1)} %down_hbm.3), custom_call_target="tpu_custom_call" | custom-call | flops 4831838208 | bytes 23068672 | tf_op jit(solution)/shard_map/pallas_call | solution.py:177
  243.1 19.7 %all-to-all-done.3 = bf16[16,16,4096]{2,1,0:T(8,128)(2,1)S(1)} async-done(((bf16[16,16,4096]{2,1,0:T(8,128)(2,1)}), bf16[16,16,4096]{2,1,0:T(8,128)(2,1)S(1)}, u32[]{:S(2)}, u32[]{:S(2)}) %all-to-all-start.3) | async-done | bytes 2097184 | tf_op jit(solution)/shard_map/all_to_all | solution.py:362
  264.1 3.7 %all-to-all-start.1 = ((bf16[16,16,4096]{2,1,0:T(8,128)(2,1)}), bf16[16,16,4096]{2,1,0:T(8,128)(2,1)S(1)}, u32[]{:S(2)}, u32[]{:S(2)}) async-start(bf16[16,16,4096]{2,1,0:T(8,128)(2,1)} %bitcast.40), calls=%async_computation.1 | async-start | bytes 4194304 | tf_op jit(solution)/shard_map/all_to_all | solution.py:362
  273.0 46.9 %all-to-all-done.1 = bf16[16,16,4096]{2,1,0:T(8,128)(2,1)S(1)} async-done(((bf16[16,16,4096]{2,1,0:T(8,128)(2,1)}), bf16[16,16,4096]{2,1,0:T(8,128)(2,1)S(1)}, u32[]{:S(2)}, u32[]{:S(2)}) %all-to-all-start.1) | async-done | bytes 2097184 | tf_op jit(solution)/shard_map/all_to_all | solution.py:362
  319.9 2.7 shard_map.101
  (64 shorter events, 35.4 us)
Async XLA Ops:
  2.3 14.3 %collective-permute-start.7 = (s32[128,4]{1,0:T(8,128)S(1)}, s32[128,4]{1,0:T(8,128)S(1)}, u32[]{:S(2)}, u32[]{:S(2)}) collective-permute-start(s32[128,4]{1,0:T(8,128)S(1)} %pad_add_fusion), channel_id=1, source_target_pairs={{0,24},{4,28},{8,16},{12,20},{16,8},{20,12},{24,0},{28,4},{1,25},{... | collective-permute-start | bytes 6152 | tf_op jit(solution)/shard_map/ppermute | solution.py:356
  9.2 14.1 %collective-permute-start.5 = (bf16[3,128,512]{2,1,0:T(8,128)(2,1)}, bf16[3,128,512]{2,1,0:T(8,128)(2,1)S(1)}, u32[]{:S(2)}, u32[]{:S(2)}) collective-permute-start(bf16[3,128,512]{2,1,0:T(8,128)(2,1)} %shard_map.96), channel_id=1, source_target_pairs={{0,24},{4,28},{8,16},{12,20},{16,8},{20,12},{24,0},{28,4},{1,25},{... | collective-permute-start | bytes 1179656 | tf_op jit(solution)/shard_map/ppermute | solution.py:359
  12.0 18.4 %collective-permute-start = (bf16[3,128,512]{2,1,0:T(8,128)(2,1)}, bf16[3,128,512]{2,1,0:T(8,128)(2,1)S(1)}, u32[]{:S(2)}, u32[]{:S(2)}) collective-permute-start(bf16[3,128,512]{2,1,0:T(8,128)(2,1)} %get-tuple-element.35), channel_id=1, source_target_pairs={{0,4},{4,0},{8,12},{12,8},{16,20},{20,16},{24,28},{28,24},{1,5},{5... | collective-permute-start | bytes 1179656 | tf_op jit(solution)/shard_map/ppermute | solution.py:359
  13.7 28.2 %collective-permute-start.1 = (bf16[3,128,512]{2,1,0:T(8,128)(2,1)}, bf16[3,128,512]{2,1,0:T(8,128)(2,1)S(1)}, u32[]{:S(2)}, u32[]{:S(2)}) collective-permute-start(bf16[3,128,512]{2,1,0:T(8,128)(2,1)} %get-tuple-element.36), channel_id=1, source_target_pairs={{0,8},{4,12},{8,0},{12,4},{16,24},{20,28},{24,16},{28,20},{1,9},{5... | collective-permute-start | bytes 1179656 | tf_op jit(solution)/shard_map/ppermute | solution.py:359
  13.7 37.4 %collective-permute-start.2 = (bf16[3,128,512]{2,1,0:T(8,128)(2,1)}, bf16[3,128,512]{2,1,0:T(8,128)(2,1)S(1)}, u32[]{:S(2)}, u32[]{:S(2)}) collective-permute-start(bf16[3,128,512]{2,1,0:T(8,128)(2,1)} %get-tuple-element.37), channel_id=1, source_target_pairs={{0,12},{4,8},{8,4},{12,0},{16,28},{20,24},{24,20},{28,16},{1,13},{... | collective-permute-start | bytes 1179656 | tf_op jit(solution)/shard_map/ppermute | solution.py:359
  16.6 34.5 %collective-permute-start.3 = (bf16[3,128,512]{2,1,0:T(8,128)(2,1)}, bf16[3,128,512]{2,1,0:T(8,128)(2,1)S(1)}, u32[]{:S(2)}, u32[]{:S(2)}) collective-permute-start(bf16[3,128,512]{2,1,0:T(8,128)(2,1)} %get-tuple-element.38), channel_id=1, source_target_pairs={{0,16},{4,20},{8,24},{12,28},{16,0},{20,4},{24,8},{28,12},{1,17},{... | collective-permute-start | bytes 1179656 | tf_op jit(solution)/shard_map/ppermute | solution.py:359
  23.3 48.7 %collective-permute-start.4 = (bf16[3,128,512]{2,1,0:T(8,128)(2,1)}, bf16[3,128,512]{2,1,0:T(8,128)(2,1)S(1)}, u32[]{:S(2)}, u32[]{:S(2)}) collective-permute-start(bf16[3,128,512]{2,1,0:T(8,128)(2,1)} %get-tuple-element.39), channel_id=1, source_target_pairs={{0,20},{4,16},{8,28},{12,24},{16,4},{20,0},{24,12},{28,8},{1,21},{... | collective-permute-start | bytes 1179656 | tf_op jit(solution)/shard_map/ppermute | solution.py:359
  30.4 41.6 %collective-permute-start.6 = (bf16[3,128,512]{2,1,0:T(8,128)(2,1)}, bf16[3,128,512]{2,1,0:T(8,128)(2,1)S(1)}, u32[]{:S(2)}, u32[]{:S(2)}) collective-permute-start(bf16[3,128,512]{2,1,0:T(8,128)(2,1)} %get-tuple-element.40), channel_id=1, source_target_pairs={{0,28},{4,24},{8,20},{12,16},{16,12},{20,8},{24,4},{28,0},{1,29},{... | collective-permute-start | bytes 1179656 | tf_op jit(solution)/shard_map/ppermute | solution.py:359
  33.0 76.8 %copy-start = (bf16[1,128,4096]{2,1,0:T(8,128)(2,1)S(1)}, bf16[1,128,4096]{2,1,0:T(8,128)(2,1)}, u32[]{:S(2)}) copy-start(bf16[1,128,4096]{2,1,0:T(8,128)(2,1)} %param.9) | copy-start | bytes 3145732
  33.0 76.8 %copy-start.3 = (f32[4096]{0:T(1024)S(1)}, f32[4096]{0:T(1024)}, u32[]{:S(2)}) copy-start(f32[4096]{0:T(1024)} %param.10) | copy-start | bytes 49156
  79.1 12.1 %collective-permute-start.8 = (bf16[128,512]{1,0:T(8,128)(2,1)}, bf16[128,512]{1,0:T(8,128)(2,1)S(1)}, u32[]{:S(2)}, u32[]{:S(2)}) collective-permute-start(bf16[128,512]{1,0:T(8,128)(2,1)} %get-tuple-element.50), channel_id=1, source_target_pairs={{0,4},{4,0},{8,12},{12,8},{16,20},{20,16},{24,28},{28,24},{1,5},{5... | collective-permute-start | bytes 393224 | tf_op jit(solution)/shard_map/ppermute | solution.py:359
  79.7 14.5 %collective-permute-start.9 = (bf16[128,512]{1,0:T(8,128)(2,1)}, bf16[128,512]{1,0:T(8,128)(2,1)S(1)}, u32[]{:S(2)}, u32[]{:S(2)}) collective-permute-start(bf16[128,512]{1,0:T(8,128)(2,1)} %get-tuple-element.51), channel_id=1, source_target_pairs={{0,8},{4,12},{8,0},{12,4},{16,24},{20,28},{24,16},{28,20},{1,9},{5... | collective-permute-start | bytes 393224 | tf_op jit(solution)/shard_map/ppermute | solution.py:359
  87.2 10.7 %collective-permute-start.10 = (bf16[128,512]{1,0:T(8,128)(2,1)}, bf16[128,512]{1,0:T(8,128)(2,1)S(1)}, u32[]{:S(2)}, u32[]{:S(2)}) collective-permute-start(bf16[128,512]{1,0:T(8,128)(2,1)} %get-tuple-element.52), channel_id=1, source_target_pairs={{0,12},{4,8},{8,4},{12,0},{16,28},{20,24},{24,20},{28,16},{1,13},{... | collective-permute-start | bytes 393224 | tf_op jit(solution)/shard_map/ppermute | solution.py:359
  88.2 9.8 %collective-permute-start.11 = (bf16[128,512]{1,0:T(8,128)(2,1)}, bf16[128,512]{1,0:T(8,128)(2,1)S(1)}, u32[]{:S(2)}, u32[]{:S(2)}) collective-permute-start(bf16[128,512]{1,0:T(8,128)(2,1)} %get-tuple-element.53), channel_id=1, source_target_pairs={{0,16},{4,20},{8,24},{12,28},{16,0},{20,4},{24,8},{28,12},{1,17},{... | collective-permute-start | bytes 393224 | tf_op jit(solution)/shard_map/ppermute | solution.py:359
  91.2 18.7 %collective-permute-start.12 = (bf16[128,512]{1,0:T(8,128)(2,1)}, bf16[128,512]{1,0:T(8,128)(2,1)S(1)}, u32[]{:S(2)}, u32[]{:S(2)}) collective-permute-start(bf16[128,512]{1,0:T(8,128)(2,1)} %get-tuple-element.54), channel_id=1, source_target_pairs={{0,20},{4,16},{8,28},{12,24},{16,4},{20,0},{24,12},{28,8},{1,21},{... | collective-permute-start | bytes 393224 | tf_op jit(solution)/shard_map/ppermute | solution.py:359
  91.2 18.7 %collective-permute-start.13 = (bf16[128,512]{1,0:T(8,128)(2,1)}, bf16[128,512]{1,0:T(8,128)(2,1)S(1)}, u32[]{:S(2)}, u32[]{:S(2)}) collective-permute-start(bf16[128,512]{1,0:T(8,128)(2,1)} %get-tuple-element.55), channel_id=1, source_target_pairs={{0,24},{4,28},{8,16},{12,20},{16,8},{20,12},{24,0},{28,4},{1,25},{... | collective-permute-start | bytes 393224 | tf_op jit(solution)/shard_map/ppermute | solution.py:359
  94.2 15.6 %collective-permute-start.14 = (bf16[128,512]{1,0:T(8,128)(2,1)}, bf16[128,512]{1,0:T(8,128)(2,1)S(1)}, u32[]{:S(2)}, u32[]{:S(2)}) collective-permute-start(bf16[128,512]{1,0:T(8,128)(2,1)} %get-tuple-element.56), channel_id=1, source_target_pairs={{0,28},{4,24},{8,20},{12,16},{16,12},{20,8},{24,4},{28,0},{1,29},{... | collective-permute-start | bytes 393224 | tf_op jit(solution)/shard_map/ppermute | solution.py:359
  112.8 23.1 %collective-permute-start.15 = (bf16[128,4096]{1,0:T(8,128)(2,1)S(1)}, bf16[128,4096]{1,0:T(8,128)(2,1)S(1)}, u32[]{:S(2)}, u32[]{:S(2)}) collective-permute-start(bf16[128,4096]{1,0:T(8,128)(2,1)S(1)} %get-tuple-element.61), channel_id=1, source_target_pairs={{0,24},{4,28},{8,16},{12,20},{16,8},{20,12},{24,0},{28,4},{1,25},{... | collective-permute-start | bytes 3145736 | tf_op jit(solution)/shard_map/ppermute | solution.py:356
  137.9 57.4 %all-to-all-start.2 = ((bf16[16,16,4096]{2,1,0:T(8,128)(2,1)}), bf16[16,16,4096]{2,1,0:T(8,128)(2,1)S(1)}, u32[]{:S(2)}, u32[]{:S(2)}) async-start(bf16[16,16,4096]{2,1,0:T(8,128)(2,1)} %bitcast.39), calls=%async_computation.2 | async-start | bytes 4194304 | tf_op jit(solution)/shard_map/all_to_all | solution.py:362
  195.3 34.1 %all-to-all-start = ((bf16[16,16,4096]{2,1,0:T(8,128)(2,1)}), bf16[16,16,4096]{2,1,0:T(8,128)(2,1)}, u32[]{:S(2)}, u32[]{:S(2)}) async-start(bf16[16,16,4096]{2,1,0:T(8,128)(2,1)} %bitcast.38), calls=%async_computation | async-start | bytes 4194304 | tf_op jit(solution)/shard_map/all_to_all | solution.py:362
  229.4 33.4 %all-to-all-start.3 = ((bf16[16,16,4096]{2,1,0:T(8,128)(2,1)}), bf16[16,16,4096]{2,1,0:T(8,128)(2,1)S(1)}, u32[]{:S(2)}, u32[]{:S(2)}) async-start(bf16[16,16,4096]{2,1,0:T(8,128)(2,1)} %bitcast.41), calls=%async_computation.3 | async-start | bytes 4194304 | tf_op jit(solution)/shard_map/all_to_all | solution.py:362
  264.1 55.8 %all-to-all-start.1 = ((bf16[16,16,4096]{2,1,0:T(8,128)(2,1)}), bf16[16,16,4096]{2,1,0:T(8,128)(2,1)S(1)}, u32[]{:S(2)}, u32[]{:S(2)}) async-start(bf16[16,16,4096]{2,1,0:T(8,128)(2,1)} %bitcast.40), calls=%async_computation.1 | async-start | bytes 4194304 | tf_op jit(solution)/shard_map/all_to_all | solution.py:362
  270.0 49.9 %copy-start.1 = (bf16[128,4096]{1,0:T(8,128)(2,1)S(1)}, bf16[128,4096]{1,0:T(8,128)(2,1)}, u32[]{:S(2)}) copy-start(bf16[128,4096]{1,0:T(8,128)(2,1)} %get-tuple-element.62.stream_ref) | copy-start | bytes 3145732
  271.5 48.4 %collective-permute-start.16 = (bf16[128,4096]{1,0:T(8,128)(2,1)}, bf16[128,4096]{1,0:T(8,128)(2,1)}, u32[]{:S(2)}, u32[]{:S(2)}) collective-permute-start(bf16[128,4096]{1,0:T(8,128)(2,1)} %fusion), channel_id=1, source_target_pairs={{0,24},{4,28},{8,16},{12,20},{16,8},{20,12},{24,0},{28,4},{1,25},{... | collective-permute-start | bytes 3145736 | tf_op jit(solution)/shard_map/ppermute | solution.py:356
  (4 other events, 5.4 us)
